TPU v7x, 128 devices: a whole 4x4x4 slice. The times are simulated.
128 devices in a mesh: wide: 16 (over x, z_lo, core), narrow: 8 (over z_hi, y).
Axes of the slice: x: 4, y: 4, z: 4 (z_hi: 2, z_lo: 2; z = z_hi * 2 + z_lo), core: 2. Of those that a mesh axis runs over, the one named last changes fastest.
Arguments:
- saturation: float32 [256, 128, 1024], P('wide', None, 'narrow'), may hold values from 0.05 to 0.95
- pressure: float32 [256, 128, 1024], P('wide', None, 'narrow'), may hold values from -6 to 6
- rock_class: int32 [256, 128, 1024], P('wide', None, 'narrow'), may hold values from 0 to 15
- rock_table: float32 [3, 16], replicated, may hold values from 0.2 to 5
- well_columns: int32 [64], replicated, may hold values from 0 to 131071
- well_rates: float32 [64], replicated, may hold values from 2 to 8
- residual: float32 [256, 128, 1024], P(None, 'wide', 'narrow'), may hold values from -7 to 7
Outputs:
- sat_new: float32 [256, 128, 1024], P('wide', None, 'narrow')
- precond: float32 [256, 128, 1024], P(None, 'wide', 'narrow')
Inputs may be any that keep to these rules, and one draw needn't show every extreme that they name: `well_columns`: a well with column c injects into every depth layer at row c // 1024, column c % 1024; columns may repeat.
All inputs are finite; a program needn't handle non-finite values.
Results may differ from a plain program's by a relative error of at most 0.0003.
Values sent between devices are 32-bit elements; how exact they have to be, the bound alone decides.
No kernel may reach another device: no remote copies, remote signals or barrier semaphores. Data moves between devices by JAX's collectives and lax.ppermute only.
A program may use at most 64 MiB of HBM per device.

v0:
```python
import functools

import jax
import jax.numpy as jnp
from jax import lax
from jax.experimental import pallas as pl
from jax.experimental.pallas import tpu as pltpu
from jax.sharding import PartitionSpec as P


SWEEPS = 6
compress = 0.05
relax = 0.8
gravity = 0.5
courant = 0.5
tiny = 1e-06

F32 = jnp.float32
HIGH = lax.Precision.HIGHEST
PARAMS = pltpu.CompilerParams(vmem_limit_bytes=16 * 1024 * 1024)


def harmonic(low, high):
    return 2.0 * low * high / (low + high)


def sub_iota():
    return lax.broadcasted_iota(jnp.int32, (8, 128), 0)


def lane_iota():
    return lax.broadcasted_iota(jnp.int32, (8, 128), 1)


def lane_pick(tile, index):
    return jnp.take_along_axis(tile, jnp.full((8, 128), index, jnp.int32), axis=1)


def lane_take(tile, index):
    return jnp.take_along_axis(tile, index, axis=1, mode="promise_in_bounds")


def mobility(wg, og, s):
    water = wg * s * s
    return water, water + og * (1.0 - s) * (1.0 - s)


def lane_table(table, n):
    row = jnp.concatenate([table[n : n + 1, :], jnp.zeros((1, 112), F32)], axis=1)
    return jnp.broadcast_to(row, (8, 128))


def spread(tile, lane):
    return jnp.broadcast_to(tile[:, lane : lane + 1], (8, 128))


def call(kernel, outs, scratch=(), aliases=None, out_specs=None, in_specs=None):
    def run(*args):
        return pl.pallas_call(
            kernel,
            out_shape=[jax.ShapeDtypeStruct(shape, F32) for shape in outs],
            in_specs=in_specs or [pl.BlockSpec(memory_space=pltpu.VMEM)] * len(args),
            out_specs=out_specs or [pl.BlockSpec(memory_space=pltpu.VMEM)] * len(outs),
            scratch_shapes=list(scratch),
            input_output_aliases=aliases or {},
            compiler_params=PARAMS,
        )(*args)

    return run


def faces_kernel(
    place, sat_in, press_in, rock_in, sat, press, kinds, face_a, face_b, pack_a, pack_b, rock, sem
):
    lane = lane_iota()
    depth, rows_all, _ = sat.shape
    groups = 8
    each = rows_all // groups
    copies = []
    for g in range(groups):
        part = pl.ds(g * each, each)
        for n, (src, dst) in enumerate(((rock_in, rock), (sat_in, sat), (press_in, press))):
            copies.append(
                pltpu.make_async_copy(src.at[:, part, :], dst.at[:, part, :], sem.at[g * 3 + n])
            )
            copies[-1].start()
    even_row = place[2] % 2 == 0
    even_col = place[0] % 2 == 0

    def rows(step, carry):
        at = pl.ds(pl.multiple_of(step * 8, 8), 8)
        first = jnp.zeros((8, 128), F32)
        last = jnp.zeros((8, 128), F32)
        for d in range(depth):
            kind = rock[d, at, :].astype(F32) + 1.0
            kinds[d, at, :] = kind
            fields = (kind, sat[d, at, :], press[d, at, :])
            for n, field in enumerate(fields):
                spot = n * depth + d
                turned = pltpu.roll(field, spot + 1, 1)
                first = jnp.where(lane == spot + 1, turned, first)
                last = jnp.where(lane == spot, turned, last)
                if d == 0:
                    face_a[n, at, :] = field
                if d + 1 == depth:
                    low = face_a[n, at, :]
                    face_a[n, at, :] = jnp.where(even_row, field, low)
                    face_b[n, at, :] = jnp.where(even_row, low, field)
        first = pltpu.roll(first, 127, 1)
        pack_a[at, :] = jnp.where(even_col, last, first)
        pack_b[at, :] = jnp.where(even_col, first, last)
        return carry

    def two_rows(step, carry):
        return rows(2 * step + 1, rows(2 * step, carry))

    for g in range(groups):
        for copy in copies[g * 3 : g * 3 + 3]:
            copy.wait()
        lax.fori_loop(g * (each // 16), (g + 1) * (each // 16), two_rows, 0)


def rock_of(tables, kind, s):
    index = jnp.maximum(kind.astype(jnp.int32) - 1, 0)
    k, wg, og = [lane_take(table, index) for table in tables]
    water, both = mobility(wg, og, s)
    return jnp.where(kind > 0.5, k, 0.0), water / both


def columns_of(tables, depth, pack):
    lane = lane_iota()
    kind = jnp.where(lane < depth, pack, 0.0)
    k, f = rock_of(tables, kind, pltpu.roll(pack, 128 - depth, 1))
    return [pltpu.roll(pack, 128 - 2 * depth, 1), k, f]


def lookup_kernel(
    bricks, place, table, kinds, sat, pack_a, pack_b, columns, rates, residual,
    perm, wgain, ogain, frac, own_a, own_b, source, rest,
):
    depth, rows_all, cols = sat.shape
    tables = [lane_table(table, n) for n in range(3)]
    entries = [jnp.broadcast_to(table[2:3, m : m + 1], (8, 128)) for m in range(16)]

    def rows(step, carry):
        at = pl.ds(pl.multiple_of(step * 8, 8), 8)
        for d in range(depth):
            kind = kinds[d, at, :].astype(jnp.int32) - 1
            k = lane_take(tables[0], kind)
            wg = lane_take(tables[1], kind)
            values = entries
            for bit in range(4):
                taken = (kind & (1 << bit)) != 0
                values = [
                    jnp.where(taken, values[m + 1], values[m]) for m in range(0, len(values), 2)
                ]
            og = values[0]
            water, both = mobility(wg, og, sat[d, at, :])
            perm[d, at, :] = k
            wgain[d, at, :] = wg
            ogain[d, at, :] = og
            frac[d, at, :] = water / both
        for pack, own in ((pack_a, own_a), (pack_b, own_b)):
            for n, field in enumerate(columns_of(tables, depth, pack[at, :])):
                own[n, at, :] = field
        return carry

    lax.fori_loop(0, rows_all // 8, rows, 0)

    def add(step, sums):
        at = step * 8
        return tuple(s + residual[at + n] for n, s in enumerate(sums))

    sums = lax.fori_loop(0, residual.shape[0] // 8, add, (jnp.zeros((8, 128), F32),) * 8)
    total = sum(sums[1:], sums[0])
    rest[...] = jnp.broadcast_to(jnp.sum(total, keepdims=True), (8, 128))

    wells = columns.shape[1]
    spot = lax.broadcasted_iota(jnp.int32, (rows_all, wells), 0)
    apart = columns[...] - spot * (cols * bricks)
    in_row = jnp.where((apart >= 0) & (apart < cols * bricks), 1.0, 0.0)
    number = columns[...]
    well_col = number & (cols * bricks - 1) if (cols * bricks) & (cols * bricks - 1) == 0 else number % (cols * bricks)
    spot = lax.broadcasted_iota(jnp.int32, (cols, wells), 0)
    in_col = jnp.where(well_col - place[0] * cols == spot, rates[...], 0.0)
    source[...] = lax.dot_general(
        in_row, in_col, (((1,), (1,)), ((), ())), precision=HIGH, preferred_element_type=F32
    )


def flows(low, high, lift, keep=None):
    total = low[1] * high[1] / (low[1] + high[1]) * (low[0] - high[0] + lift)
    if keep is not None:
        total = jnp.where(keep, total, 0.0)
    return total, total * jnp.where(total > 0, low[2], high[2])


def flow_kernel(
    place, table, press, perm, frac, face_a, face_b, own_a, own_b, got_a, got_b,
    source, rest, net, ahead, message, qp, wp, rq, rw,
):
    lane = lane_iota()
    sub = sub_iota()
    depth, rows_all, _ = perm.shape
    tiles = rows_all // 8
    even_row = place[2] % 2 == 0
    even_col = place[0] % 2 == 0
    half = lane >> 1
    odd = (lane & 1) == 1
    tables = [lane_table(table, n) for n in range(3)]

    def edge(step, carry):
        at = pl.ds(pl.multiple_of(step * 8, 8), 8)

        mine_a, mine_b = [[ref[n, at, :] for n in range(3)] for ref in (own_a, own_b)]
        other_a, other_b = [columns_of(tables, depth, ref[at, :]) for ref in (got_a, got_b)]

        def choose(one, two):
            return [jnp.where(even_col, a, b) for a, b in zip(one, two)]

        left = flows(choose(other_b, other_a), choose(mine_b, mine_a), 0.0)
        right = flows(choose(mine_a, mine_b), choose(other_a, other_b), 0.0)
        for out, low, high in zip((qp, wp), left, right):
            out[at, :] = jnp.where(
                odd,
                jnp.take_along_axis(low, half, axis=1),
                jnp.take_along_axis(high, half, axis=1),
            )
        return carry

    def two_edges(step, carry):
        return edge(2 * step + 1, edge(2 * step, carry))

    lax.fori_loop(0, tiles // 2, two_edges, 0)
    rq[...] = jnp.zeros(rq.shape, F32)
    rw[...] = jnp.zeros(rw.shape, F32)

    def rows(step, top):
        begin = pl.multiple_of(step * 8, 8)
        at = pl.ds(begin, 8)
        beyond = pl.ds(pl.multiple_of(jnp.minimum(begin + 8, rows_all - 8), 8), 8)
        inner = (sub < 7) | (step < tiles - 1)
        edge_q, edge_w = qp[at, :], wp[at, :]
        kind, s, p = [jnp.where(even_row, face_b[n, at, :], face_a[n, at, :]) for n in range(3)]
        below = [p, *rock_of(tables, kind, s)]
        kind, s, p = [jnp.where(even_row, face_a[n, at, :], face_b[n, at, :]) for n in range(3)]
        above = [p, *rock_of(tables, kind, s)]
        cur = [ref[0, at, :] for ref in (press, perm, frac)]
        depth_q, depth_w = flows(below, cur, gravity)
        told = jnp.where(
            (lane >= depth) & (lane < 2 * depth), spread(source[at, :], 127), 0.0
        )
        for d in range(depth):
            nxt = [ref[d + 1, at, :] for ref in (press, perm, frac)] if d + 1 < depth else above
            q, w = flows(cur, nxt, gravity)
            net_sum = w - depth_w
            out = jnp.maximum(q, 0.0) - jnp.minimum(depth_q, 0.0)
            depth_q, depth_w = q, w
            up = [
                pltpu.roll(jnp.where(sub == 0, ref[d, beyond, :], x), 7, 0)
                for ref, x in zip((press, perm, frac), cur)
            ]
            q, w = flows(cur, up, 0.0, inner)
            q_roll, w_roll = pltpu.roll(q, 1, 0), pltpu.roll(w, 1, 0)
            low_q = jnp.where(sub == 0, rq[d], q_roll)
            low_w = jnp.where(sub == 0, rw[d], w_roll)
            rq[d] = q_roll
            rw[d] = w_roll
            net_sum = net_sum + (w - low_w)
            out = out + (jnp.maximum(q, 0.0) - jnp.minimum(low_q, 0.0))
            q, w = flows(cur, [pltpu.roll(x, 127, 1) for x in cur], 0.0)
            side_q = pltpu.roll(edge_q, 127 - 2 * d, 1)
            side_w = pltpu.roll(edge_w, 127 - 2 * d, 1)
            low_q = jnp.where(lane == 0, side_q, pltpu.roll(q, 1, 1))
            low_w = jnp.where(lane == 0, side_w, pltpu.roll(w, 1, 1))
            q = jnp.where(lane == 127, side_q, q)
            w = jnp.where(lane == 127, side_w, w)
            net_sum = 2.0 * (net_sum + (w - low_w))
            net[d, at, :] = net_sum
            told = jnp.where(lane == d, pltpu.roll(net_sum, d + 1, 1), told)
            out = out + (jnp.maximum(q, 0.0) - jnp.minimum(low_q, 0.0))
            top = jnp.maximum(top, out)
            cur = nxt
        ahead[at, :] = told
        return top

    top = lax.fori_loop(0, tiles, rows, jnp.zeros((8, 128), F32))

    message[...] = jnp.where(
        lax.broadcasted_iota(jnp.int32, message.shape, 1) == 0,
        2.0 * jnp.max(top),
        rest[0:1, :],
    )


def update_kernel(
    place, gathered, table, sat, net, source, perm, wgain, ogain, got_a, got_b, beside,
    new, chunks, cell_sum, row_sum, col_sum,
):
    lane = lane_iota()
    depth, rows_all, _ = sat.shape
    tiles = rows_all // 8
    stride = (depth + 1) * 8
    spot = lax.broadcasted_iota(jnp.int32, gathered.shape, 1)
    top = jnp.max(jnp.where(spot == 0, gathered[...], 0.0), keepdims=True)
    step_size = jnp.broadcast_to(courant / (top + tiny), (8, 128))
    even_col = place[0] % 2 == 0
    tables = [lane_table(table, n) for n in range(3)]

    def coefficient(k, wg, og, s):
        return k * (wg * s * s + og * (1.0 - s) * (1.0 - s))

    def rows(step, carry):
        at = pl.ds(pl.multiple_of(step * 8, 8), 8)
        begin = step * stride
        add = step_size * source[at, :]
        total = jnp.zeros((8, 128), F32)
        first = jnp.zeros((8, 128), F32)
        for d in range(depth):
            s = sat[d, at, :] - step_size * net[d, at, :] + add
            new[d, at, :] = s
            c = coefficient(perm[d, at, :], wgain[d, at, :], ogain[d, at, :], s)
            chunks[pl.ds(pl.multiple_of(begin + d * 8, 8), 8), :] = c
            total = total + c
            first = jnp.where(lane == d, pltpu.roll(c, d, 1) if d else c, first)
        cell_sum[at, :] = total
        tile = jnp.where(even_col, got_b[at, :], got_a[at, :])
        flow = beside[at, :]
        kind = jnp.where(lane < depth, tile, 0.0)
        index = jnp.maximum(kind.astype(jnp.int32) - 1, 0)
        k, wg, og = [lane_take(each, index) for each in tables]
        s = pltpu.roll(tile, 128 - depth, 1) - step_size * flow
        s = s + step_size * pltpu.roll(flow, 128 - depth, 1)
        c = coefficient(jnp.where(kind > 0.5, k, 0.0), wg, og, s)
        col_sum[at, :] = jnp.where(lane < depth, harmonic(c, first), 0.0)
        return carry

    def two_rows(step, carry):
        return rows(2 * step + 1, rows(2 * step, carry))

    lax.fori_loop(0, tiles // 2, two_rows, 0)
    row_sum[0:8, :] = jnp.zeros((8, 128), F32)
    for p in range(1, tiles):
        total = jnp.zeros((8, 128), F32)
        for half in range(depth // 8):
            low = chunks[pl.ds((p - 1) * stride + half * 64 + 7, 8, stride=8), :]
            high = chunks[pl.ds(p * stride + half * 64, 8, stride=8), :]
            total = total + harmonic(low, high)
        row_sum[p * 8 : p * 8 + 8, :] = total
    brick = lax.broadcasted_iota(jnp.int32, (rows_all, 128), 0) // 8
    spot = lax.broadcasted_iota(jnp.int32, (rows_all, 128), 1)
    total = jnp.zeros((1, 128), F32)
    for n, part in enumerate((cell_sum, row_sum, col_sum)):
        each = jnp.sum(part[...], axis=1, keepdims=True)
        placed = jnp.where(spot == n * 16 + brick, each, 0.0)
        total = total + jnp.sum(placed, axis=0, keepdims=True)
    for p in range(tiles):
        chunks[p * stride + depth * 8 : (p + 1) * stride, :] = jnp.broadcast_to(total, (8, 128))


def relax_kernel(
    depth, place, got, residual, new, values, row_a, row_b, message, new_out, fd, fr, fc, gain, base, sem
):
    leave = pltpu.make_async_copy(new, new_out, sem.at[0])
    leave.start()
    lane = lane_iota()
    sub = sub_iota()
    layers = residual.shape[0] // 8
    parts = layers // depth
    zero = jnp.zeros((8, 128), F32)
    fd[0:8, :] = zero
    values[layers * 8 :, :] = jnp.zeros((64, 128), F32)
    fc[layers * 8 :, :] = jnp.zeros((64, 128), F32)
    even_row = place[2] % 2 == 0

    def half_face(low, high):
        return low * high / (low + high)

    def part(w, carry):
        below, total = carry
        begin = w * (depth + 1) * 8
        place_w = w * depth * 8
        after = jnp.minimum(w + 1, parts - 1) * (depth + 1) * 8
        c = got[pl.ds(pl.multiple_of(begin, 8), 8), :]
        for d in range(depth):
            here = pl.ds(pl.multiple_of(place_w + d * 8, 8), 8)
            if d + 1 < depth:
                c_next = got[pl.ds(pl.multiple_of(begin + d * 8 + 8, 8), 8), :]
                above = half_face(c, c_next)
            else:
                c_next = got[pl.ds(pl.multiple_of(after, 8), 8), :]
                above = jnp.where(w + 1 < parts, half_face(c, c_next), 0.0)
            row = jnp.where(sub == 0, 0.0, half_face(pltpu.roll(c, 1, 0), c))
            col = jnp.where(lane == 0, 0.0, half_face(pltpu.roll(c, 1, 1), c))
            diag = (
                (0.5 * compress) * c + below + above
                + row + pltpu.roll(row, 7, 0) + col + pltpu.roll(col, 127, 1)
            )
            scale = relax / diag
            fd[pl.ds(pl.multiple_of(place_w + d * 8 + 8, 8), 8), :] = above
            fr[here, :] = row
            fc[here, :] = col
            gain[here, :] = scale
            first = (0.5 * scale) * residual[here, :]
            base[here, :] = first
            values[here, :] = first
            c, below = c_next, above
        total = total + got[pl.ds(pl.multiple_of(begin + depth * 8, 8), 8), :]
        return below, total

    def build(step, carry):
        return part(2 * step + 1, part(2 * step, carry))

    _, total = lax.fori_loop(0, parts // 2, build, (zero, zero))

    block = 32

    def sweep(number, carry):
        def some(step, prev):
            begin = step * (block * 8)
            v = values[pl.ds(pl.multiple_of(begin, 8), 8), :]
            for n in range(block):
                here = pl.ds(pl.multiple_of(begin + n * 8, 8), 8)
                above = pl.ds(pl.multiple_of(begin + n * 8 + 8, 8), 8)
                v_next = values[above, :]
                row = fr[here, :]
                col = fc[here, :]
                total = fd[here, :] * prev + fd[above, :] * v_next
                total = total + (row * pltpu.roll(v, 1, 0) + pltpu.roll(row * v, 7, 0))
                total = total + (col * pltpu.roll(v, 1, 1) + pltpu.roll(col * v, 127, 1))
                values[here, :] = ((1.0 - relax) * v + base[here, :]) + gain[here, :] * total
                prev, v = v, v_next
            return prev

        lax.fori_loop(0, layers // block, some, zero)
        return carry

    lax.fori_loop(0, SWEEPS - 1, sweep, 0)

    for w in range(parts):
        for half in range(depth // 8):
            at = w * (depth + 1) * 8 + half * 64
            spot = w * depth + half * 8
            pairs = []
            for row in (0, 7):
                c = got[pl.ds(at + row, 8, stride=8), :]
                v = values[pl.ds(spot * 8 + row, 8, stride=8), :]
                pairs.append((c * v, c))
            for n in range(2):
                low, high = pairs[0][n], pairs[1][n]
                rows = slice(n * layers + spot, n * layers + spot + 8)
                row_a[rows, :] = jnp.where(even_row, high, low)
                row_b[rows, :] = jnp.where(even_row, low, high)

    quarters = layers // 64
    per_tile = 64 // depth
    peers = message.shape[0] // (quarters * 16 + 8)

    def pack(quarter, carry):
        packed = [zero, zero]
        for l in range(64):
            part = quarter * per_tile + l // depth
            c = got[pl.ds(pl.multiple_of(part * (depth + 1) * 8 + l % depth * 8, 8), 8), :]
            v = values[pl.ds(pl.multiple_of(quarter * 512 + l * 8, 8), 8), :]
            spot = (2 * l + 2) % 128
            mark = (lane == 2 * l + 1) | (lane == spot)
            for n, tile in enumerate((c * v, c)):
                turned = pltpu.roll(tile, spot, 1) if spot else tile
                packed[n] = jnp.where(mark, turned, packed[n])
        for peer in range(peers):
            for n in range(2):
                begin = peer * (quarters * 16 + 8) + (n * quarters + quarter) * 8
                message[pl.ds(pl.multiple_of(begin, 8), 8), :] = packed[n]
        return carry

    lax.fori_loop(0, quarters, pack, 0)
    for peer in range(peers):
        begin = peer * (quarters * 16 + 8) + quarters * 16
        message[begin : begin + 8, :] = total
    leave.wait()


def coarse_kernel(count, place, news, gathered, out):
    lane = lane_iota()
    sub = sub_iota()
    inside = lane < count
    width = gathered.shape[0] // count
    stride = news.shape[0] // width
    sums = jnp.zeros((8, 128), F32)
    for k in range(width):
        sums = jnp.where(sub == k, news[(k + 1) * stride - 8 : (k + 1) * stride, :], sums)
    cells = jnp.where(inside, sums, 0.0)
    low_row = jnp.where(inside, pltpu.roll(sums, 128 - 16, 1), 0.0)
    low_col = jnp.where(inside, pltpu.roll(sums, 128 - 32, 1), 0.0)
    low_row = jnp.where(lane == 0, 0.0, low_row)
    low_col = jnp.where(sub == 0, 0.0, low_col)
    high_row = pltpu.roll(low_row, 127, 1)
    high_col = pltpu.roll(low_col, 7, 0)
    diagonal = jnp.where(inside, compress * cells + low_row + high_row + low_col + high_col, 1.0)
    rhs = jnp.zeros((8, 128), F32)
    for p in range(count):
        rhs = jnp.where(lane == p, spread(gathered[p * width : p * width + width, :], 1), rhs)

    def line(tile, k):
        return jnp.broadcast_to(tile[k : k + 1, :], (8, 128))

    zero = jnp.zeros((8, 128), F32)
    main, lower, upper, right = [], [], [], []
    for k in range(width):
        row = jnp.where(sub == k, line(diagonal, k), zero)
        if k > 0:
            row = jnp.where(sub == k - 1, -line(low_col, k), row)
        if k + 1 < width:
            row = jnp.where(sub == k + 1, -line(low_col, k + 1), row)
        main.append(row)
        lower.append(jnp.where(sub == k, -line(low_row, k), zero))
        upper.append(jnp.where(sub == k, -line(high_row, k), zero))
        right.append(line(rhs, k))

    def eliminate(main, others):
        main = list(main)
        others = [list(rows) for rows in others]
        for k in range(width):
            inverse = 1.0 / line(main[k], k)
            main[k] = main[k] * inverse
            for rows in others:
                rows[k] = rows[k] * inverse
            for j in range(width):
                if j != k:
                    factor = line(main[j], k)
                    main[j] = main[j] - factor * main[k]
                    for rows in others:
                        rows[j] = rows[j] - factor * rows[k]
        return others

    stride = 1
    while stride < count:
        solved = eliminate(main, [lower, upper, right])
        back = [[pltpu.roll(x, stride, 1) for x in rows] for rows in solved]
        ahead = [[pltpu.roll(x, 128 - stride, 1) for x in rows] for rows in solved]
        new_lower, new_upper, new_main, new_right = [], [], [], []
        for k in range(width):
            lo, up, mid, rt = zero, zero, main[k], right[k]
            for j in [k] if stride == 1 else range(width):
                a = line(lower[k], j)
                b = line(upper[k], j)
                if 2 * stride < count:
                    lo = lo - a * back[0][j]
                    up = up - b * ahead[1][j]
                mid = mid - a * back[1][j] - b * ahead[0][j]
                rt = rt - a * back[2][j] - b * ahead[2][j]
            new_lower.append(lo)
            new_upper.append(up)
            new_main.append(mid)
            new_right.append(rt)
        lower, upper, main, right = new_lower, new_upper, new_main, new_right
        stride *= 2
    (right,) = eliminate(main, [right])
    mine = zero
    for k in range(width):
        mine = jnp.where(place[0] == k, right[k], mine)
    out[...] = lane_pick(mine, place[2])


def final_kernel(depth, place, got, values, row_a, row_b, news, coarse, result, packs, out, sem):
    lane = lane_iota()
    sub = sub_iota()
    layers = out.shape[0] // 8
    quarters = layers // 64
    per_tile = 64 // depth
    add = coarse[...]
    even_row = place[2] % 2 == 0
    stride = quarters * 16 + 8
    left = pl.multiple_of(jnp.maximum(place[0] - 1, 0) * stride, 8)
    right = pl.multiple_of(jnp.minimum(place[0] + 1, place[1] - 1) * stride, 8)
    odd = (lane & 1) == 1
    has_left = odd & (place[0] > 0)
    has_right = jnp.logical_not(odd) & (place[0] + 1 < place[1])
    for n in range(quarters * 2):
        low = news[pl.ds(left + n * 8, 8), :]
        high = pltpu.roll(news[pl.ds(right + n * 8, 8), :], 126, 1)
        packs[n * 8 : n * 8 + 8, :] = jnp.where(has_left, low, jnp.where(has_right, high, 0.0))
    ends = (lane == 0) | (lane == 127)

    def some(quarter, carry):
        sides = [
            packs[pl.ds(pl.multiple_of((n * quarters + quarter) * 8, 8), 8), :] for n in range(2)
        ]
        for l in range(64):
            g = quarter * 64 + l
            part = quarter * per_tile + l // depth
            here = pl.ds(pl.multiple_of(g * 8, 8), 8)
            c = got[pl.ds(pl.multiple_of(part * (depth + 1) * 8 + l % depth * 8, 8), 8), :]
            v = values[here, :]
            pair = []
            for n, tile in enumerate((c * v, c)):
                at = pl.ds(n * layers + g, 1)
                low = jnp.where(even_row, row_b[at, :], row_a[at, :])
                high = jnp.where(even_row, row_a[at, :], row_b[at, :])
                tile = tile + jnp.where(sub == 0, low, jnp.where(sub == 7, high, 0.0))
                tile = tile + jnp.where(ends, pltpu.roll(sides[n], 127 - 2 * l, 1), 0.0)
                pair.append(tile)
            out[here, :] = pair[0] / pair[1] + add
        leave(quarter).start()
        return carry

    def leave(quarter):
        part = pl.ds(pl.multiple_of(quarter * 512, 512), 512)
        return pltpu.make_async_copy(out.at[part, :], result.at[part, :], sem.at[quarter])

    lax.fori_loop(0, quarters, some, 0)
    for quarter in range(quarters):
        leave(quarter).wait()


def partners(array, axis, odd):
    count = lax.axis_size(axis)
    pairs = [(i, i + 1) for i in range(odd, count - 1, 2)]
    return lax.ppermute(array, axis, pairs + [(j, i) for i, j in pairs])


def forward(array, axis):
    count = lax.axis_size(axis)
    return lax.ppermute(array, axis, [(i, i + 1) for i in range(count - 1)])


def shards(saturation, pressure, rock_class, rock_table, well_columns, well_rates, residual):
    depth, rows_all, cols = saturation.shape
    layers, brick_rows, _ = residual.shape
    wide, narrow = lax.axis_size("wide"), lax.axis_size("narrow")
    block = (depth, rows_all, cols)
    plane = (rows_all, cols)
    place = jnp.stack(
        [lax.axis_index("narrow"), jnp.int32(narrow), lax.axis_index("wide")]
    ).astype(jnp.int32)
    vmem = pl.BlockSpec(memory_space=pltpu.VMEM)
    smem = pl.BlockSpec(memory_space=pltpu.SMEM)
    far = pl.BlockSpec(memory_space=pltpu.HBM)

    sat, press, kinds, face_a, face_b, pack_a, pack_b = call(
        faces_kernel,
        [block] * 3 + [(3,) + plane] * 2 + [plane] * 2,
        scratch=[pltpu.VMEM(block, jnp.int32), pltpu.SemaphoreType.DMA((24,))],
        in_specs=[smem] + [far] * 3,
    )(
        place,
        *(
            pltpu.with_memory_space_constraint(array, pltpu.HBM)
            for array in (saturation, pressure, rock_class)
        ),
    )
    perm, wgain, ogain, frac, own_a, own_b, source, rest = call(
        functools.partial(lookup_kernel, narrow),
        [block] * 4 + [(3,) + plane] * 2 + [plane, (8, 128)],
        in_specs=[smem] + [vmem] * 8,
    )(
        place, rock_table, kinds, sat, pack_a, pack_b,
        well_columns.reshape(1, -1), well_rates.reshape(1, -1), residual,
    )
    got_face_a = partners(face_a, "wide", 0)
    got_face_b = partners(face_b, "wide", 1)
    got_pack_b = partners(pack_b, "narrow", 1)
    got_pack_a = partners(pack_a, "narrow", 0)
    net, ahead, message = call(
        flow_kernel,
        [block, plane, (wide * narrow, 128)],
        scratch=[pltpu.VMEM(plane, F32)] * 2 + [pltpu.VMEM((depth, 8, cols), F32)] * 2,
        in_specs=[smem] + [vmem] * 12,
    )(
        place, rock_table, press, perm, frac, got_face_a, got_face_b, own_a, own_b,
        got_pack_a, got_pack_b, source, rest,
    )
    beside = forward(ahead, "narrow")
    gathered = lax.all_to_all(message, ("wide", "narrow"), 0, 0, tiled=True)
    chunk_rows = wide * (depth + 1) * 8
    new, chunks = call(
        update_kernel,
        [block, (chunk_rows, 128)],
        scratch=[pltpu.VMEM(plane, F32)] * 3,
        in_specs=[smem] + [vmem] * 11,
    )(
        place, gathered, rock_table, sat, net, source, perm, wgain, ogain, got_pack_a, got_pack_b,
        beside,
    )
    got = lax.all_to_all(chunks, "wide", 0, 0, tiled=True)
    message_rows = narrow * (layers // 4 + 8)
    values, row_a, row_b, message, sat_new = call(
        functools.partial(relax_kernel, depth),
        [(layers * 8 + 64, 128)] + [(2 * layers, 128)] * 2 + [(message_rows, 128), block],
        scratch=[pltpu.VMEM((layers * 8 + 64, 128), F32)] * 5 + [pltpu.SemaphoreType.DMA((1,))],
        in_specs=[smem] + [vmem] * 3,
        out_specs=[vmem] * 4 + [far],
    )(place, got, residual.reshape(layers * 8, 128), new)
    got_row_a = partners(row_a, "wide", 0)
    got_row_b = partners(row_b, "wide", 1)
    news = lax.all_to_all(message, "narrow", 0, 0, tiled=True)
    (coarse,) = call(
        functools.partial(coarse_kernel, wide), [(8, 128)], in_specs=[smem, vmem, vmem]
    )(place, news, gathered)
    (precond,) = call(
        functools.partial(final_kernel, depth),
        [(layers * 8, 128)],
        scratch=[
            pltpu.VMEM((layers // 4, 128), F32),
            pltpu.VMEM((layers * 8, 128), F32),
            pltpu.SemaphoreType.DMA((layers // 64,)),
        ],
        in_specs=[smem] + [vmem] * 6,
        out_specs=[far],
    )(place, got, values, got_row_a, got_row_b, news, coarse)
    return (sat_new, precond.reshape(layers, brick_rows, cols))


def solution(mesh):
    placed = (
        P("wide", None, "narrow"),
        P("wide", None, "narrow"),
        P("wide", None, "narrow"),
        P(),
        P(),
        P(),
        P(None, "wide", "narrow"),
    )
    return jax.shard_map(
        shards,
        mesh=mesh,
        in_specs=placed,
        out_specs=(P("wide", None, "narrow"), P(None, "wide", "narrow")),
        check_vma=False,
    )
```

profile of v0, /device:TPU:1, one launch (start us, length us, event | category | flops | bytes accessed | tf_op | source)
XLA Modules:
  0.0 98.7 jit_solution(543278581322582698)
XLA Ops:
  0.6 0.1 pad_add_fusion.place
  0.7 3.7 %shard_map.86 = (f32[16,128,128]{2,1,0:T(8,128)S(1)}, f32[16,128,128]{2,1,0:T(8,128)S(1)}, f32[16,128,128]{2,1,0:T(8,128)S(1)}, f32[3,128,128]{2,1,0:T(8,128)S(1...) custom-call(s32[3]{0:T(128)S(1)} %pad_add_fusion.place, f32[16,128,128]{2,1,0:T(8,128)} %sat_in.1, ...), custom_call_target="tpu_custom_call" | custom-call | tf_op jit(solution)/shard_map/pallas_call | solution.py:59
  4.5 1.5 %collective-permute-start = (f32[3,128,128]{2,1,0:T(8,128)S(1)}, f32[3,128,128]{2,1,0:T(8,128)S(1)}, u32[]{:S(2)}, u32[]{:S(2)}) collective-permute-start(f32[3,128,128]{2,1,0:T(8,128)S(1)} %get-tuple-element.34), channel_id=1, source_target_pairs={{0,8},{16,24},{32,40},{48,56},{64,72},{80,88},{96,104},{112,120},{... | collective-permute-start | bytes 589832 | tf_op jit(solution)/shard_map/ppermute | solution.py:619
  5.9 3.6 %collective-permute-start.1 = (f32[3,128,128]{2,1,0:T(8,128)S(1)}, f32[3,128,128]{2,1,0:T(8,128)S(1)}, u32[]{:S(2)}, u32[]{:S(2)}) collective-permute-start(f32[3,128,128]{2,1,0:T(8,128)S(1)} %get-tuple-element.35), channel_id=1, source_target_pairs={{8,16},{24,32},{40,48},{56,64},{72,80},{88,96},{104,112},{16,8},{3... | collective-permute-start | bytes 589832 | tf_op jit(solution)/shard_map/ppermute | solution.py:619
  9.5 1.4 %collective-permute-start.2 = (f32[128,128]{1,0:T(8,128)S(1)}, f32[128,128]{1,0:T(8,128)S(1)}, u32[]{:S(2)}, u32[]{:S(2)}) collective-permute-start(f32[128,128]{1,0:T(8,128)S(1)} %get-tuple-element.30.pack_a), channel_id=1, source_target_pairs={{0,1},{2,3},{4,5},{6,7},{1,0},{3,2},{5,4},{7,6},{8,9},{10,11},{12,... | collective-permute-start | bytes 196616 | tf_op jit(solution)/shard_map/ppermute | solution.py:619
  10.9 0.7 collective-permute-start.3
  11.6 3.9 %shard_map.87 = (f32[16,128,128]{2,1,0:T(8,128)S(1)}, f32[16,128,128]{2,1,0:T(8,128)S(1)}, f32[16,128,128]{2,1,0:T(8,128)S(1)}, f32[16,128,128]{2,1,0:T(8,128)S(...) custom-call(s32[3]{0:T(128)S(1)} %pad_add_fusion.place, ...), custom_call_target="tpu_custom_call" | custom-call | tf_op jit(solution)/shard_map/pallas_call | solution.py:59
  15.5 0.0 collective-permute-done.2.got_a
  15.5 0.0 collective-permute-done.3.got_b
  15.5 0.0 collective-permute-done.1.face_b
  15.5 6.7 %shard_map.88 = (f32[16,128,128]{2,1,0:T(8,128)S(1)}, f32[128,128]{1,0:T(8,128)S(1)}, f32[128,128]{1,0:T(8,128)S(1)}) custom-call(s32[3]{0:T(128)S(1)} %pad_add_fusion.place, f32[3,16]{1,0:T(4,128)S(1)} %copy-done.1, f32[16,128,128]{2,1,0:T(8,128)S(1)} %get-tuple-element.27.press, f32[16,128,128]{2,1,0:T(8,128)S(1)} %get-tuple-element.32.perm, ...), custom_call_target="tpu_custom_call" | custom-call | tf_op jit(solution)/shard_map/pallas_call | solution.py:59
  22.2 5.5 %collective-permute-start.4 = (f32[128,128]{1,0:T(8,128)S(1)}, f32[128,128]{1,0:T(8,128)S(1)}, u32[]{:S(2)}, u32[]{:S(2)}) collective-permute-start(f32[128,128]{1,0:T(8,128)S(1)} %get-tuple-element.44), channel_id=1, source_target_pairs={{0,1},{1,2},{2,3},{3,4},{4,5},{5,6},{6,7},{8,9},{9,10},{10,11},{11... | collective-permute-start | bytes 196616 | tf_op jit(solution)/shard_map/ppermute | solution.py:624
  27.7 21.6 %all_to_all.33 = f32[128,1,128]{2,1,0:T(1,128)S(1)} all-to-all(f32[128,1,128]{2,1,0:T(1,128)S(1)} %bitcast.23), channel_id=1, replica_groups=mesh['wide'=16,'narrow'=8] {'wide','narrow'}, dimensions={0} | all-to-all | bytes 131072 | tf_op jit(solution)/shard_map/all_to_all | solution.py:674
  49.3 0.0 collective-permute-done.4.beside
  49.3 2.0 %shard_map.89 = (f32[16,128,128]{2,1,0:T(8,128)S(1)}, f32[2176,128]{1,0:T(8,128)S(1)}) custom-call(s32[3]{0:T(128)S(1)} %pad_add_fusion.place, f32[128,128]{1,0:T(8,128)S(1)} %bitcast.20, f32[3,16]{1,0:T(4,128)S(1)} %copy-done.1, f32[16,128,128]{2,1,0:T(8,128)S(1)} %get-tuple-element.29.sat, f32[16,128,128]{2,1,0:T(8,128)S(1)} %get-tuple-element.41.net, ...), custom_call_target="tpu_custom_call" | custom-call | tf_op jit(solution)/shard_map/pallas_call | solution.py:59
  51.2 20.1 %all_to_all.34 = f32[16,136,128]{2,1,0:T(8,128)S(1)} all-to-all(f32[16,136,128]{2,1,0:T(8,128)S(1)} %bitcast.19), channel_id=1, replica_groups=mesh['wide'=16,'narrow'=8] {'wide'}, dimensions={0} | all-to-all | bytes 2228224 | tf_op jit(solution)/shard_map/all_to_all | solution.py:685
  71.4 8.8 %shard_map.90 = (f32[2112,128]{1,0:T(8,128)S(1)}, f32[512,128]{1,0:T(8,128)S(1)}, f32[512,128]{1,0:T(8,128)S(1)}, f32[576,128]{1,0:T(8,128)S(1)}, f32[16,128,128]{2,1,0:T(8,128)}) custom-call(s32[3]{0:T(128)S(1)} %pad_add_fusion.place, f32[2176,128]{1,0:T(8,128)S(1)} %bitcast.14, f32[2048,128]{1,0:T(8,128)S(1)} %bitcast.16, ...), custom_call_target="tpu_custom_call" | custom-call | tf_op jit(solution)/shard_map/pallas_call | solution.py:59
  80.2 0.5 collective-permute-start.5
  80.6 2.3 %collective-permute-start.6 = (f32[512,128]{1,0:T(8,128)S(1)}, f32[512,128]{1,0:T(8,128)S(1)}, u32[]{:S(2)}, u32[]{:S(2)}) collective-permute-start(f32[512,128]{1,0:T(8,128)S(1)} %get-tuple-element.50), channel_id=1, source_target_pairs={{8,16},{24,32},{40,48},{56,64},{72,80},{88,96},{104,112},{16,8},{3... | collective-permute-start | bytes 786440 | tf_op jit(solution)/shard_map/ppermute | solution.py:619
  82.9 11.9 %all_to_all.35 = f32[8,72,128]{2,1,0:T(8,128)S(1)} all-to-all(f32[8,72,128]{2,1,0:T(8,128)S(1)} %bitcast.22), channel_id=1, replica_groups=mesh['wide'=16,'narrow'=8] {'narrow'}, dimensions={0} | all-to-all | bytes 589824 | tf_op jit(solution)/shard_map/all_to_all | solution.py:696
  94.8 1.7 %shard_map.91.coarse = f32[8,128]{1,0:T(8,128)S(1)} custom-call(s32[3]{0:T(128)S(1)} %pad_add_fusion.place, f32[576,128]{1,0:T(8,128)S(1)} %bitcast.17, f32[128,128]{1,0:T(8,128)S(1)} %bitcast.21), custom_call_target="tpu_custom_call" | custom-call | tf_op jit(solution)/shard_map/pallas_call | solution.py:59
  96.5 0.0 collective-permute-done.5.row_a
  96.5 0.0 collective-permute-done.6.row_b
  96.5 2.2 %shard_map.92 = f32[2048,128]{1,0:T(8,128)} custom-call(s32[3]{0:T(128)S(1)} %pad_add_fusion.place, f32[2176,128]{1,0:T(8,128)S(1)} %bitcast.15, f32[2112,128]{1,0:T(8,128)S(1)} %get-tuple-element.48.values, f32[512,128]{1,0:T(8,128)S(1)} %collective-permute-done.5.row_a, f32[512,128]{1,0:T(8,128)S(1)} %collective-permute-done.6.row_b, ...), custom_call_target="tpu_custom_call" | custom-call | tf_op jit(solution)/shard_map/pallas_call | solution.py:59
  (9 shorter events, 0.0 us)
Async XLA Ops:
  0.7 10.8 %copy-start = (f32[256,8,128]{2,1,0:T(8,128)S(1)}, f32[256,8,128]{2,1,0:T(8,128)}, u32[]{:S(2)}) copy-start(f32[256,8,128]{2,1,0:T(8,128)} %residual.1) | copy-start | bytes 3145732
  0.7 10.8 %copy-start.1 = (f32[3,16]{1,0:T(4,128)S(1)}, f32[3,16]{1,0:T(4,128)}, u32[]{:S(2)}) copy-start(f32[3,16]{1,0:T(4,128)} %table.5) | copy-start | bytes 580
  0.7 10.8 %copy-start.2 = (s32[64]{0:T(128)S(1)}, s32[64]{0:T(128)}, u32[]{:S(2)}) copy-start(s32[64]{0:T(128)} %param.11) | copy-start | bytes 772
  0.7 10.9 %copy-start.3 = (f32[64]{0:T(128)S(1)}, f32[64]{0:T(128)}, u32[]{:S(2)}) copy-start(f32[64]{0:T(128)} %param.12) | copy-start | bytes 772
  4.5 11.0 %collective-permute-start = (f32[3,128,128]{2,1,0:T(8,128)S(1)}, f32[3,128,128]{2,1,0:T(8,128)S(1)}, u32[]{:S(2)}, u32[]{:S(2)}) collective-permute-start(f32[3,128,128]{2,1,0:T(8,128)S(1)} %get-tuple-element.34), channel_id=1, source_target_pairs={{0,8},{16,24},{32,40},{48,56},{64,72},{80,88},{96,104},{112,120},{... | collective-permute-start | bytes 589832 | tf_op jit(solution)/shard_map/ppermute | solution.py:619
  5.9 9.6 %collective-permute-start.1 = (f32[3,128,128]{2,1,0:T(8,128)S(1)}, f32[3,128,128]{2,1,0:T(8,128)S(1)}, u32[]{:S(2)}, u32[]{:S(2)}) collective-permute-start(f32[3,128,128]{2,1,0:T(8,128)S(1)} %get-tuple-element.35), channel_id=1, source_target_pairs={{8,16},{24,32},{40,48},{56,64},{72,80},{88,96},{104,112},{16,8},{3... | collective-permute-start | bytes 589832 | tf_op jit(solution)/shard_map/ppermute | solution.py:619
  9.5 6.0 %collective-permute-start.2 = (f32[128,128]{1,0:T(8,128)S(1)}, f32[128,128]{1,0:T(8,128)S(1)}, u32[]{:S(2)}, u32[]{:S(2)}) collective-permute-start(f32[128,128]{1,0:T(8,128)S(1)} %get-tuple-element.30.pack_a), channel_id=1, source_target_pairs={{0,1},{2,3},{4,5},{6,7},{1,0},{3,2},{5,4},{7,6},{8,9},{10,11},{12,... | collective-permute-start | bytes 196616 | tf_op jit(solution)/shard_map/ppermute | solution.py:619
  10.9 4.6 %collective-permute-start.3 = (f32[128,128]{1,0:T(8,128)S(1)}, f32[128,128]{1,0:T(8,128)S(1)}, u32[]{:S(2)}, u32[]{:S(2)}) collective-permute-start(f32[128,128]{1,0:T(8,128)S(1)} %get-tuple-element.31.pack_b), channel_id=1, source_target_pairs={{1,2},{3,4},{5,6},{2,1},{4,3},{6,5},{9,10},{11,12},{13,14},{10,9},... | collective-permute-start | bytes 196616 | tf_op jit(solution)/shard_map/ppermute | solution.py:619
  22.2 27.0 %collective-permute-start.4 = (f32[128,128]{1,0:T(8,128)S(1)}, f32[128,128]{1,0:T(8,128)S(1)}, u32[]{:S(2)}, u32[]{:S(2)}) collective-permute-start(f32[128,128]{1,0:T(8,128)S(1)} %get-tuple-element.44), channel_id=1, source_target_pairs={{0,1},{1,2},{2,3},{3,4},{4,5},{5,6},{6,7},{8,9},{9,10},{10,11},{11... | collective-permute-start | bytes 196616 | tf_op jit(solution)/shard_map/ppermute | solution.py:624
  80.2 16.3 %collective-permute-start.5 = (f32[512,128]{1,0:T(8,128)S(1)}, f32[512,128]{1,0:T(8,128)S(1)}, u32[]{:S(2)}, u32[]{:S(2)}) collective-permute-start(f32[512,128]{1,0:T(8,128)S(1)} %get-tuple-element.49), channel_id=1, source_target_pairs={{0,8},{16,24},{32,40},{48,56},{64,72},{80,88},{96,104},{112,120},{... | collective-permute-start | bytes 786440 | tf_op jit(solution)/shard_map/ppermute | solution.py:619
  80.6 15.9 %collective-permute-start.6 = (f32[512,128]{1,0:T(8,128)S(1)}, f32[512,128]{1,0:T(8,128)S(1)}, u32[]{:S(2)}, u32[]{:S(2)}) collective-permute-start(f32[512,128]{1,0:T(8,128)S(1)} %get-tuple-element.50), channel_id=1, source_target_pairs={{8,16},{24,32},{40,48},{56,64},{72,80},{88,96},{104,112},{16,8},{3... | collective-permute-start | bytes 786440 | tf_op jit(solution)/shard_map/ppermute | solution.py:619
where the time goes:
time: 99 us; the launch traced here: 98.7 us
  blocking collectives  53.6 us (54%)
  Pallas kernels  29.1 us (29%)
  starting transfers between devices  15.2 us (15%)
    pallas_call x7, Pallas kernels, run(): pl.pallas_call(kernel, out_shape=[jax.ShapeDtypeStruct(shape, F32) for sh...  29.1 us
    all_to_all x1, blocking collectives, shards(): gathered = lax.all_to_all(message, ('wide', 'narrow'), 0, 0, tiled=True)  21.6 us
    all_to_all x1, blocking collectives, shards(): got = lax.all_to_all(chunks, 'wide', 0, 0, tiled=True)  20.1 us
    all_to_all x1, blocking collectives, shards(): news = lax.all_to_all(message, 'narrow', 0, 0, tiled=True)  11.9 us
    ppermute x6, starting transfers between devices, partners(): return lax.ppermute(array, axis, pairs + [(j, i) for i, j in pairs])  9.77 us
    ppermute x1, starting transfers between devices, forward(): return lax.ppermute(array, axis, [(i, i + 1) for i in range(count - 1)])  5.45 us
  transfers between devices with their start and end apart: 7, of which 0 were waited for; matrix products, arithmetic and copies ran while one was open for 0% of the time, Pallas kernels for 6%

commit v1 on v0

--- a/solution.py
+++ b/solution.py
@@ -165,7 +165,10 @@
                 own[n, at, :] = field
         return carry
 
-    lax.fori_loop(0, rows_all // 8, rows, 0)
+    def two_rows(step, carry):
+        return rows(2 * step + 1, rows(2 * step, carry))
+
+    lax.fori_loop(0, rows_all // 16, two_rows, 0)
 
     def add(step, sums):
         at = step * 8
@@ -409,11 +412,13 @@
         return below, total
 
     def build(step, carry):
-        return part(2 * step + 1, part(2 * step, carry))
-
-    _, total = lax.fori_loop(0, parts // 2, build, (zero, zero))
-
-    block = 32
+        for n in range(4):
+            carry = part(4 * step + n, carry)
+        return carry
+
+    _, total = lax.fori_loop(0, parts // 4, build, (zero, zero))
+
+    block = 256
 
     def sweep(number, carry):
         def some(step, prev):

time: 99 us -> 96.6 us (0.976)
  Pallas kernels: 29.1 us -> 26.1 us
    pallas_call x7, Pallas kernels: 29.1 us -> 26.1 us  [run(): pl.pallas_call(kernel, out_shape=[jax.ShapeDtypeStruct(shape, F32) for sh...]
  transfers between devices with their start and end apart: 7 -> 7, of which waited for: 0 -> 0; matrix products, arithmetic and copies ran while one was open for 0% -> 0% of each run, Pallas kernels for 6% -> 5%
where the time goes in v1:
time: 96.6 us; the launch traced here: 96.3 us
  blocking collectives  54.1 us (56%)
  Pallas kernels  26.1 us (27%)
  starting transfers between devices  15.2 us (16%)
    pallas_call x7, Pallas kernels, run(): pl.pallas_call(kernel, out_shape=[jax.ShapeDtypeStruct(shape, F32) for sh...  26.1 us
    all_to_all x1, blocking collectives, shards(): gathered = lax.all_to_all(message, ('wide', 'narrow'), 0, 0, tiled=True)  22.1 us
    all_to_all x1, blocking collectives, shards(): got = lax.all_to_all(chunks, 'wide', 0, 0, tiled=True)  20.1 us
    all_to_all x1, blocking collectives, shards(): news = lax.all_to_all(message, 'narrow', 0, 0, tiled=True)  11.9 us
    ppermute x6, starting transfers between devices, partners(): return lax.ppermute(array, axis, pairs + [(j, i) for i, j in pairs])  9.77 us
    ppermute x1, starting transfers between devices, forward(): return lax.ppermute(array, axis, [(i, i + 1) for i in range(count - 1)])  5.45 us
  transfers between devices with their start and end apart: 7, of which 0 were waited for; matrix products, arithmetic and copies ran while one was open for 0% of the time, Pallas kernels for 5%

profile of v1, /device:TPU:1, one launch (start us, length us, event | category | flops | bytes accessed | tf_op | source)
XLA Modules:
  0.0 96.3 jit_solution(17611867330158494094)
XLA Ops:
  0.6 0.1 pad_add_fusion.place
  0.7 3.7 %shard_map.86 = (f32[16,128,128]{2,1,0:T(8,128)S(1)}, f32[16,128,128]{2,1,0:T(8,128)S(1)}, f32[16,128,128]{2,1,0:T(8,128)S(1)}, f32[3,128,128]{2,1,0:T(8,128)S(1...) custom-call(s32[3]{0:T(128)S(1)} %pad_add_fusion.place, f32[16,128,128]{2,1,0:T(8,128)} %sat_in.1, ...), custom_call_target="tpu_custom_call" | custom-call | tf_op jit(solution)/shard_map/pallas_call | solution.py:59
  4.5 1.5 %collective-permute-start = (f32[3,128,128]{2,1,0:T(8,128)S(1)}, f32[3,128,128]{2,1,0:T(8,128)S(1)}, u32[]{:S(2)}, u32[]{:S(2)}) collective-permute-start(f32[3,128,128]{2,1,0:T(8,128)S(1)} %get-tuple-element.34), channel_id=1, source_target_pairs={{0,8},{16,24},{32,40},{48,56},{64,72},{80,88},{96,104},{112,120},{... | collective-permute-start | bytes 589832 | tf_op jit(solution)/shard_map/ppermute | solution.py:624
  5.9 3.6 %collective-permute-start.1 = (f32[3,128,128]{2,1,0:T(8,128)S(1)}, f32[3,128,128]{2,1,0:T(8,128)S(1)}, u32[]{:S(2)}, u32[]{:S(2)}) collective-permute-start(f32[3,128,128]{2,1,0:T(8,128)S(1)} %get-tuple-element.35), channel_id=1, source_target_pairs={{8,16},{24,32},{40,48},{56,64},{72,80},{88,96},{104,112},{16,8},{3... | collective-permute-start | bytes 589832 | tf_op jit(solution)/shard_map/ppermute | solution.py:624
  9.5 1.4 %collective-permute-start.2 = (f32[128,128]{1,0:T(8,128)S(1)}, f32[128,128]{1,0:T(8,128)S(1)}, u32[]{:S(2)}, u32[]{:S(2)}) collective-permute-start(f32[128,128]{1,0:T(8,128)S(1)} %get-tuple-element.30.pack_a), channel_id=1, source_target_pairs={{0,1},{2,3},{4,5},{6,7},{1,0},{3,2},{5,4},{7,6},{8,9},{10,11},{12,... | collective-permute-start | bytes 196616 | tf_op jit(solution)/shard_map/ppermute | solution.py:624
  10.9 0.7 collective-permute-start.3
  11.6 3.3 %shard_map.87 = (f32[16,128,128]{2,1,0:T(8,128)S(1)}, f32[16,128,128]{2,1,0:T(8,128)S(1)}, f32[16,128,128]{2,1,0:T(8,128)S(1)}, f32[16,128,128]{2,1,0:T(8,128)S(...) custom-call(s32[3]{0:T(128)S(1)} %pad_add_fusion.place, ...), custom_call_target="tpu_custom_call" | custom-call | tf_op jit(solution)/shard_map/pallas_call | solution.py:59
  14.9 0.0 collective-permute-done.2.got_a
  14.9 0.0 collective-permute-done.3.got_b
  14.9 0.0 collective-permute-done.face_a
  15.0 6.7 %shard_map.88 = (f32[16,128,128]{2,1,0:T(8,128)S(1)}, f32[128,128]{1,0:T(8,128)S(1)}, f32[128,128]{1,0:T(8,128)S(1)}) custom-call(s32[3]{0:T(128)S(1)} %pad_add_fusion.place, f32[3,16]{1,0:T(4,128)S(1)} %copy-done.1, f32[16,128,128]{2,1,0:T(8,128)S(1)} %get-tuple-element.27.press, f32[16,128,128]{2,1,0:T(8,128)S(1)} %get-tuple-element.32.perm, ...), custom_call_target="tpu_custom_call" | custom-call | tf_op jit(solution)/shard_map/pallas_call | solution.py:59
  21.7 5.5 %collective-permute-start.4 = (f32[128,128]{1,0:T(8,128)S(1)}, f32[128,128]{1,0:T(8,128)S(1)}, u32[]{:S(2)}, u32[]{:S(2)}) collective-permute-start(f32[128,128]{1,0:T(8,128)S(1)} %get-tuple-element.44), channel_id=1, source_target_pairs={{0,1},{1,2},{2,3},{3,4},{4,5},{5,6},{6,7},{8,9},{9,10},{10,11},{11... | collective-permute-start | bytes 196616 | tf_op jit(solution)/shard_map/ppermute | solution.py:629
  27.1 22.1 %all_to_all.33 = f32[128,1,128]{2,1,0:T(1,128)S(1)} all-to-all(f32[128,1,128]{2,1,0:T(1,128)S(1)} %bitcast.23), channel_id=1, replica_groups=mesh['wide'=16,'narrow'=8] {'wide','narrow'}, dimensions={0} | all-to-all | bytes 131072 | tf_op jit(solution)/shard_map/all_to_all | solution.py:679
  49.3 0.0 collective-permute-done.4.beside
  49.3 2.0 %shard_map.89 = (f32[16,128,128]{2,1,0:T(8,128)S(1)}, f32[2176,128]{1,0:T(8,128)S(1)}) custom-call(s32[3]{0:T(128)S(1)} %pad_add_fusion.place, f32[128,128]{1,0:T(8,128)S(1)} %bitcast.20, f32[3,16]{1,0:T(4,128)S(1)} %copy-done.1, f32[16,128,128]{2,1,0:T(8,128)S(1)} %get-tuple-element.29.sat, f32[16,128,128]{2,1,0:T(8,128)S(1)} %get-tuple-element.41.net, ...), custom_call_target="tpu_custom_call" | custom-call | tf_op jit(solution)/shard_map/pallas_call | solution.py:59
  51.2 20.1 %all_to_all.34 = f32[16,136,128]{2,1,0:T(8,128)S(1)} all-to-all(f32[16,136,128]{2,1,0:T(8,128)S(1)} %bitcast.19), channel_id=1, replica_groups=mesh['wide'=16,'narrow'=8] {'wide'}, dimensions={0} | all-to-all | bytes 2228224 | tf_op jit(solution)/shard_map/all_to_all | solution.py:690
  71.4 6.3 %shard_map.90 = (f32[2112,128]{1,0:T(8,128)S(1)}, f32[512,128]{1,0:T(8,128)S(1)}, f32[512,128]{1,0:T(8,128)S(1)}, f32[576,128]{1,0:T(8,128)S(1)}, f32[16,128,128]{2,1,0:T(8,128)}) custom-call(s32[3]{0:T(128)S(1)} %pad_add_fusion.place, f32[2176,128]{1,0:T(8,128)S(1)} %bitcast.14, f32[2048,128]{1,0:T(8,128)S(1)} %bitcast.16, ...), custom_call_target="tpu_custom_call" | custom-call | tf_op jit(solution)/shard_map/pallas_call | solution.py:59
  77.7 0.5 collective-permute-start.5
  78.2 2.3 %collective-permute-start.6 = (f32[512,128]{1,0:T(8,128)S(1)}, f32[512,128]{1,0:T(8,128)S(1)}, u32[]{:S(2)}, u32[]{:S(2)}) collective-permute-start(f32[512,128]{1,0:T(8,128)S(1)} %get-tuple-element.50), channel_id=1, source_target_pairs={{8,16},{24,32},{40,48},{56,64},{72,80},{88,96},{104,112},{16,8},{3... | collective-permute-start | bytes 786440 | tf_op jit(solution)/shard_map/ppermute | solution.py:624
  80.5 11.9 %all_to_all.35 = f32[8,72,128]{2,1,0:T(8,128)S(1)} all-to-all(f32[8,72,128]{2,1,0:T(8,128)S(1)} %bitcast.22), channel_id=1, replica_groups=mesh['wide'=16,'narrow'=8] {'narrow'}, dimensions={0} | all-to-all | bytes 589824 | tf_op jit(solution)/shard_map/all_to_all | solution.py:701
  92.3 1.7 %shard_map.91.coarse = f32[8,128]{1,0:T(8,128)S(1)} custom-call(s32[3]{0:T(128)S(1)} %pad_add_fusion.place, f32[576,128]{1,0:T(8,128)S(1)} %bitcast.17, f32[128,128]{1,0:T(8,128)S(1)} %bitcast.21), custom_call_target="tpu_custom_call" | custom-call | tf_op jit(solution)/shard_map/pallas_call | solution.py:59
  94.1 0.0 collective-permute-done.5.row_a
  94.1 0.0 collective-permute-done.6.row_b
  94.1 2.2 %shard_map.92 = f32[2048,128]{1,0:T(8,128)} custom-call(s32[3]{0:T(128)S(1)} %pad_add_fusion.place, f32[2176,128]{1,0:T(8,128)S(1)} %bitcast.15, f32[2112,128]{1,0:T(8,128)S(1)} %get-tuple-element.48.values, f32[512,128]{1,0:T(8,128)S(1)} %collective-permute-done.5.row_a, f32[512,128]{1,0:T(8,128)S(1)} %collective-permute-done.6.row_b, ...), custom_call_target="tpu_custom_call" | custom-call | tf_op jit(solution)/shard_map/pallas_call | solution.py:59
  (9 shorter events, 0.0 us)
Async XLA Ops:
  0.7 10.8 %copy-start = (f32[256,8,128]{2,1,0:T(8,128)S(1)}, f32[256,8,128]{2,1,0:T(8,128)}, u32[]{:S(2)}) copy-start(f32[256,8,128]{2,1,0:T(8,128)} %residual.1) | copy-start | bytes 3145732
  0.7 10.8 %copy-start.1 = (f32[3,16]{1,0:T(4,128)S(1)}, f32[3,16]{1,0:T(4,128)}, u32[]{:S(2)}) copy-start(f32[3,16]{1,0:T(4,128)} %table.5) | copy-start | bytes 580
  0.7 10.8 %copy-start.2 = (s32[64]{0:T(128)S(1)}, s32[64]{0:T(128)}, u32[]{:S(2)}) copy-start(s32[64]{0:T(128)} %param.11) | copy-start | bytes 772
  0.7 10.9 %copy-start.3 = (f32[64]{0:T(128)S(1)}, f32[64]{0:T(128)}, u32[]{:S(2)}) copy-start(f32[64]{0:T(128)} %param.12) | copy-start | bytes 772
  4.5 10.5 %collective-permute-start = (f32[3,128,128]{2,1,0:T(8,128)S(1)}, f32[3,128,128]{2,1,0:T(8,128)S(1)}, u32[]{:S(2)}, u32[]{:S(2)}) collective-permute-start(f32[3,128,128]{2,1,0:T(8,128)S(1)} %get-tuple-element.34), channel_id=1, source_target_pairs={{0,8},{16,24},{32,40},{48,56},{64,72},{80,88},{96,104},{112,120},{... | collective-permute-start | bytes 589832 | tf_op jit(solution)/shard_map/ppermute | solution.py:624
  5.9 9.0 %collective-permute-start.1 = (f32[3,128,128]{2,1,0:T(8,128)S(1)}, f32[3,128,128]{2,1,0:T(8,128)S(1)}, u32[]{:S(2)}, u32[]{:S(2)}) collective-permute-start(f32[3,128,128]{2,1,0:T(8,128)S(1)} %get-tuple-element.35), channel_id=1, source_target_pairs={{8,16},{24,32},{40,48},{56,64},{72,80},{88,96},{104,112},{16,8},{3... | collective-permute-start | bytes 589832 | tf_op jit(solution)/shard_map/ppermute | solution.py:624
  9.5 5.4 %collective-permute-start.2 = (f32[128,128]{1,0:T(8,128)S(1)}, f32[128,128]{1,0:T(8,128)S(1)}, u32[]{:S(2)}, u32[]{:S(2)}) collective-permute-start(f32[128,128]{1,0:T(8,128)S(1)} %get-tuple-element.30.pack_a), channel_id=1, source_target_pairs={{0,1},{2,3},{4,5},{6,7},{1,0},{3,2},{5,4},{7,6},{8,9},{10,11},{12,... | collective-permute-start | bytes 196616 | tf_op jit(solution)/shard_map/ppermute | solution.py:624
  10.9 4.1 %collective-permute-start.3 = (f32[128,128]{1,0:T(8,128)S(1)}, f32[128,128]{1,0:T(8,128)S(1)}, u32[]{:S(2)}, u32[]{:S(2)}) collective-permute-start(f32[128,128]{1,0:T(8,128)S(1)} %get-tuple-element.31.pack_b), channel_id=1, source_target_pairs={{1,2},{3,4},{5,6},{2,1},{4,3},{6,5},{9,10},{11,12},{13,14},{10,9},... | collective-permute-start | bytes 196616 | tf_op jit(solution)/shard_map/ppermute | solution.py:624
  21.7 27.6 %collective-permute-start.4 = (f32[128,128]{1,0:T(8,128)S(1)}, f32[128,128]{1,0:T(8,128)S(1)}, u32[]{:S(2)}, u32[]{:S(2)}) collective-permute-start(f32[128,128]{1,0:T(8,128)S(1)} %get-tuple-element.44), channel_id=1, source_target_pairs={{0,1},{1,2},{2,3},{3,4},{4,5},{5,6},{6,7},{8,9},{9,10},{10,11},{11... | collective-permute-start | bytes 196616 | tf_op jit(solution)/shard_map/ppermute | solution.py:629
  77.7 16.3 %collective-permute-start.5 = (f32[512,128]{1,0:T(8,128)S(1)}, f32[512,128]{1,0:T(8,128)S(1)}, u32[]{:S(2)}, u32[]{:S(2)}) collective-permute-start(f32[512,128]{1,0:T(8,128)S(1)} %get-tuple-element.49), channel_id=1, source_target_pairs={{0,8},{16,24},{32,40},{48,56},{64,72},{80,88},{96,104},{112,120},{... | collective-permute-start | bytes 786440 | tf_op jit(solution)/shard_map/ppermute | solution.py:624
  78.2 15.9 %collective-permute-start.6 = (f32[512,128]{1,0:T(8,128)S(1)}, f32[512,128]{1,0:T(8,128)S(1)}, u32[]{:S(2)}, u32[]{:S(2)}) collective-permute-start(f32[512,128]{1,0:T(8,128)S(1)} %get-tuple-element.50), channel_id=1, source_target_pairs={{8,16},{24,32},{40,48},{56,64},{72,80},{88,96},{104,112},{16,8},{3... | collective-permute-start | bytes 786440 | tf_op jit(solution)/shard_map/ppermute | solution.py:624

commit v2 on v1

--- a/solution.py
+++ b/solution.py
@@ -165,10 +165,12 @@
                 own[n, at, :] = field
         return carry
 
-    def two_rows(step, carry):
-        return rows(2 * step + 1, rows(2 * step, carry))
-
-    lax.fori_loop(0, rows_all // 16, two_rows, 0)
+    def some_rows(step, carry):
+        for n in range(8):
+            carry = rows(8 * step + n, carry)
+        return carry
+
+    lax.fori_loop(0, rows_all // 64, some_rows, 0)
 
     def add(step, sums):
         at = step * 8
@@ -338,10 +340,12 @@
         col_sum[at, :] = jnp.where(lane < depth, harmonic(c, first), 0.0)
         return carry
 
-    def two_rows(step, carry):
-        return rows(2 * step + 1, rows(2 * step, carry))
-
-    lax.fori_loop(0, tiles // 2, two_rows, 0)
+    def some_rows(step, carry):
+        for n in range(8):
+            carry = rows(8 * step + n, carry)
+        return carry
+
+    lax.fori_loop(0, tiles // 8, some_rows, 0)
     row_sum[0:8, :] = jnp.zeros((8, 128), F32)
     for p in range(1, tiles):
         total = jnp.zeros((8, 128), F32)
@@ -613,7 +617,12 @@
         part = pl.ds(pl.multiple_of(quarter * 512, 512), 512)
         return pltpu.make_async_copy(out.at[part, :], result.at[part, :], sem.at[quarter])
 
-    lax.fori_loop(0, quarters, some, 0)
+    def several(step, carry):
+        for n in range(4):
+            carry = some(4 * step + n, carry)
+        return carry
+
+    lax.fori_loop(0, quarters // 4, several, 0)
     for quarter in range(quarters):
         leave(quarter).wait()
 

time: 96.6 us -> 96.1 us (level)
  Pallas kernels: 26.1 us -> 25.1 us
where the time goes in v2:
time: 96.1 us; the launch traced here: 95.8 us
  blocking collectives  54.6 us (57%)
  Pallas kernels  25.1 us (26%)
  starting transfers between devices  15.2 us (16%)
    pallas_call x7, Pallas kernels, run(): pl.pallas_call(kernel, out_shape=[jax.ShapeDtypeStruct(shape, F32) for sh...  25.1 us
    all_to_all x1, blocking collectives, shards(): gathered = lax.all_to_all(message, ('wide', 'narrow'), 0, 0, tiled=True)  22.6 us
    all_to_all x1, blocking collectives, shards(): got = lax.all_to_all(chunks, 'wide', 0, 0, tiled=True)  20.1 us
    all_to_all x1, blocking collectives, shards(): news = lax.all_to_all(message, 'narrow', 0, 0, tiled=True)  11.9 us
    ppermute x6, starting transfers between devices, partners(): return lax.ppermute(array, axis, pairs + [(j, i) for i, j in pairs])  9.77 us
    ppermute x1, starting transfers between devices, forward(): return lax.ppermute(array, axis, [(i, i + 1) for i in range(count - 1)])  5.45 us
  transfers between devices with their start and end apart: 7, of which 0 were waited for; matrix products, arithmetic and copies ran while one was open for 0% of the time, Pallas kernels for 5%

profile of v2, /device:TPU:1, one launch (start us, length us, event | category | flops | bytes accessed | tf_op | source)
XLA Modules:
  0.0 95.8 jit_solution(6051871229594593585)
XLA Ops:
  0.6 0.1 pad_add_fusion.place
  0.7 3.7 %shard_map.86 = (f32[16,128,128]{2,1,0:T(8,128)S(1)}, f32[16,128,128]{2,1,0:T(8,128)S(1)}, f32[16,128,128]{2,1,0:T(8,128)S(1)}, f32[3,128,128]{2,1,0:T(8,128)S(1...) custom-call(s32[3]{0:T(128)S(1)} %pad_add_fusion.place, f32[16,128,128]{2,1,0:T(8,128)} %sat_in.1, ...), custom_call_target="tpu_custom_call" | custom-call | tf_op jit(solution)/shard_map/pallas_call | solution.py:59
  4.5 1.5 %collective-permute-start = (f32[3,128,128]{2,1,0:T(8,128)S(1)}, f32[3,128,128]{2,1,0:T(8,128)S(1)}, u32[]{:S(2)}, u32[]{:S(2)}) collective-permute-start(f32[3,128,128]{2,1,0:T(8,128)S(1)} %get-tuple-element.34), channel_id=1, source_target_pairs={{0,8},{16,24},{32,40},{48,56},{64,72},{80,88},{96,104},{112,120},{... | collective-permute-start | bytes 589832 | tf_op jit(solution)/shard_map/ppermute | solution.py:633
  5.9 3.6 %collective-permute-start.1 = (f32[3,128,128]{2,1,0:T(8,128)S(1)}, f32[3,128,128]{2,1,0:T(8,128)S(1)}, u32[]{:S(2)}, u32[]{:S(2)}) collective-permute-start(f32[3,128,128]{2,1,0:T(8,128)S(1)} %get-tuple-element.35), channel_id=1, source_target_pairs={{8,16},{24,32},{40,48},{56,64},{72,80},{88,96},{104,112},{16,8},{3... | collective-permute-start | bytes 589832 | tf_op jit(solution)/shard_map/ppermute | solution.py:633
  9.5 1.4 %collective-permute-start.2 = (f32[128,128]{1,0:T(8,128)S(1)}, f32[128,128]{1,0:T(8,128)S(1)}, u32[]{:S(2)}, u32[]{:S(2)}) collective-permute-start(f32[128,128]{1,0:T(8,128)S(1)} %get-tuple-element.30.pack_a), channel_id=1, source_target_pairs={{0,1},{2,3},{4,5},{6,7},{1,0},{3,2},{5,4},{7,6},{8,9},{10,11},{12,... | collective-permute-start | bytes 196616 | tf_op jit(solution)/shard_map/ppermute | solution.py:633
  10.9 0.7 collective-permute-start.3
  11.6 2.9 %shard_map.87 = (f32[16,128,128]{2,1,0:T(8,128)S(1)}, f32[16,128,128]{2,1,0:T(8,128)S(1)}, f32[16,128,128]{2,1,0:T(8,128)S(1)}, f32[16,128,128]{2,1,0:T(8,128)S(...) custom-call(s32[3]{0:T(128)S(1)} %pad_add_fusion.place, ...), custom_call_target="tpu_custom_call" | custom-call | tf_op jit(solution)/shard_map/pallas_call | solution.py:59
  14.5 0.0 collective-permute-done.2.got_a
  14.5 0.0 collective-permute-done.3.got_b
  14.5 0.0 collective-permute-done.1.face_b
  14.5 6.7 %shard_map.88 = (f32[16,128,128]{2,1,0:T(8,128)S(1)}, f32[128,128]{1,0:T(8,128)S(1)}, f32[128,128]{1,0:T(8,128)S(1)}) custom-call(s32[3]{0:T(128)S(1)} %pad_add_fusion.place, f32[3,16]{1,0:T(4,128)S(1)} %copy-done.1, f32[16,128,128]{2,1,0:T(8,128)S(1)} %get-tuple-element.27.press, f32[16,128,128]{2,1,0:T(8,128)S(1)} %get-tuple-element.32.perm, ...), custom_call_target="tpu_custom_call" | custom-call | tf_op jit(solution)/shard_map/pallas_call | solution.py:59
  21.2 5.5 %collective-permute-start.4 = (f32[128,128]{1,0:T(8,128)S(1)}, f32[128,128]{1,0:T(8,128)S(1)}, u32[]{:S(2)}, u32[]{:S(2)}) collective-permute-start(f32[128,128]{1,0:T(8,128)S(1)} %get-tuple-element.44), channel_id=1, source_target_pairs={{0,1},{1,2},{2,3},{3,4},{4,5},{5,6},{6,7},{8,9},{9,10},{10,11},{11... | collective-permute-start | bytes 196616 | tf_op jit(solution)/shard_map/ppermute | solution.py:638
  26.7 22.6 %all_to_all.33 = f32[128,1,128]{2,1,0:T(1,128)S(1)} all-to-all(f32[128,1,128]{2,1,0:T(1,128)S(1)} %bitcast.23), channel_id=1, replica_groups=mesh['wide'=16,'narrow'=8] {'wide','narrow'}, dimensions={0} | all-to-all | bytes 131072 | tf_op jit(solution)/shard_map/all_to_all | solution.py:688
  49.3 0.0 collective-permute-done.4.beside
  49.3 1.6 %shard_map.89 = (f32[16,128,128]{2,1,0:T(8,128)S(1)}, f32[2176,128]{1,0:T(8,128)S(1)}) custom-call(s32[3]{0:T(128)S(1)} %pad_add_fusion.place, f32[128,128]{1,0:T(8,128)S(1)} %bitcast.20, f32[3,16]{1,0:T(4,128)S(1)} %copy-done.1, f32[16,128,128]{2,1,0:T(8,128)S(1)} %get-tuple-element.29.sat, f32[16,128,128]{2,1,0:T(8,128)S(1)} %get-tuple-element.41.net, ...), custom_call_target="tpu_custom_call" | custom-call | tf_op jit(solution)/shard_map/pallas_call | solution.py:59
  50.8 20.1 %all_to_all.34 = f32[16,136,128]{2,1,0:T(8,128)S(1)} all-to-all(f32[16,136,128]{2,1,0:T(8,128)S(1)} %bitcast.19), channel_id=1, replica_groups=mesh['wide'=16,'narrow'=8] {'wide'}, dimensions={0} | all-to-all | bytes 2228224 | tf_op jit(solution)/shard_map/all_to_all | solution.py:699
  71.0 6.3 %shard_map.90 = (f32[2112,128]{1,0:T(8,128)S(1)}, f32[512,128]{1,0:T(8,128)S(1)}, f32[512,128]{1,0:T(8,128)S(1)}, f32[576,128]{1,0:T(8,128)S(1)}, f32[16,128,128]{2,1,0:T(8,128)}) custom-call(s32[3]{0:T(128)S(1)} %pad_add_fusion.place, f32[2176,128]{1,0:T(8,128)S(1)} %bitcast.14, f32[2048,128]{1,0:T(8,128)S(1)} %bitcast.16, ...), custom_call_target="tpu_custom_call" | custom-call | tf_op jit(solution)/shard_map/pallas_call | solution.py:59
  77.3 0.5 collective-permute-start.5
  77.8 2.3 %collective-permute-start.6 = (f32[512,128]{1,0:T(8,128)S(1)}, f32[512,128]{1,0:T(8,128)S(1)}, u32[]{:S(2)}, u32[]{:S(2)}) collective-permute-start(f32[512,128]{1,0:T(8,128)S(1)} %get-tuple-element.50), channel_id=1, source_target_pairs={{8,16},{24,32},{40,48},{56,64},{72,80},{88,96},{104,112},{16,8},{3... | collective-permute-start | bytes 786440 | tf_op jit(solution)/shard_map/ppermute | solution.py:633
  80.0 11.9 %all_to_all.35 = f32[8,72,128]{2,1,0:T(8,128)S(1)} all-to-all(f32[8,72,128]{2,1,0:T(8,128)S(1)} %bitcast.22), channel_id=1, replica_groups=mesh['wide'=16,'narrow'=8] {'narrow'}, dimensions={0} | all-to-all | bytes 589824 | tf_op jit(solution)/shard_map/all_to_all | solution.py:710
  91.9 1.7 %shard_map.91.coarse = f32[8,128]{1,0:T(8,128)S(1)} custom-call(s32[3]{0:T(128)S(1)} %pad_add_fusion.place, f32[576,128]{1,0:T(8,128)S(1)} %bitcast.17, f32[128,128]{1,0:T(8,128)S(1)} %bitcast.21), custom_call_target="tpu_custom_call" | custom-call | tf_op jit(solution)/shard_map/pallas_call | solution.py:59
  93.6 0.0 collective-permute-done.5.row_a
  93.7 0.0 collective-permute-done.6.row_b
  93.7 2.2 %shard_map.92 = f32[2048,128]{1,0:T(8,128)} custom-call(s32[3]{0:T(128)S(1)} %pad_add_fusion.place, f32[2176,128]{1,0:T(8,128)S(1)} %bitcast.15, f32[2112,128]{1,0:T(8,128)S(1)} %get-tuple-element.48.values, f32[512,128]{1,0:T(8,128)S(1)} %collective-permute-done.5.row_a, f32[512,128]{1,0:T(8,128)S(1)} %collective-permute-done.6.row_b, ...), custom_call_target="tpu_custom_call" | custom-call | tf_op jit(solution)/shard_map/pallas_call | solution.py:59
  (9 shorter events, 0.0 us)
Async XLA Ops:
  0.7 10.8 %copy-start = (f32[256,8,128]{2,1,0:T(8,128)S(1)}, f32[256,8,128]{2,1,0:T(8,128)}, u32[]{:S(2)}) copy-start(f32[256,8,128]{2,1,0:T(8,128)} %residual.1) | copy-start | bytes 3145732
  0.7 10.8 %copy-start.1 = (f32[3,16]{1,0:T(4,128)S(1)}, f32[3,16]{1,0:T(4,128)}, u32[]{:S(2)}) copy-start(f32[3,16]{1,0:T(4,128)} %table.5) | copy-start | bytes 580
  0.7 10.8 %copy-start.2 = (s32[64]{0:T(128)S(1)}, s32[64]{0:T(128)}, u32[]{:S(2)}) copy-start(s32[64]{0:T(128)} %param.11) | copy-start | bytes 772
  0.7 10.9 %copy-start.3 = (f32[64]{0:T(128)S(1)}, f32[64]{0:T(128)}, u32[]{:S(2)}) copy-start(f32[64]{0:T(128)} %param.12) | copy-start | bytes 772
  4.5 10.0 %collective-permute-start = (f32[3,128,128]{2,1,0:T(8,128)S(1)}, f32[3,128,128]{2,1,0:T(8,128)S(1)}, u32[]{:S(2)}, u32[]{:S(2)}) collective-permute-start(f32[3,128,128]{2,1,0:T(8,128)S(1)} %get-tuple-element.34), channel_id=1, source_target_pairs={{0,8},{16,24},{32,40},{48,56},{64,72},{80,88},{96,104},{112,120},{... | collective-permute-start | bytes 589832 | tf_op jit(solution)/shard_map/ppermute | solution.py:633
  5.9 8.6 %collective-permute-start.1 = (f32[3,128,128]{2,1,0:T(8,128)S(1)}, f32[3,128,128]{2,1,0:T(8,128)S(1)}, u32[]{:S(2)}, u32[]{:S(2)}) collective-permute-start(f32[3,128,128]{2,1,0:T(8,128)S(1)} %get-tuple-element.35), channel_id=1, source_target_pairs={{8,16},{24,32},{40,48},{56,64},{72,80},{88,96},{104,112},{16,8},{3... | collective-permute-start | bytes 589832 | tf_op jit(solution)/shard_map/ppermute | solution.py:633
  9.5 5.0 %collective-permute-start.2 = (f32[128,128]{1,0:T(8,128)S(1)}, f32[128,128]{1,0:T(8,128)S(1)}, u32[]{:S(2)}, u32[]{:S(2)}) collective-permute-start(f32[128,128]{1,0:T(8,128)S(1)} %get-tuple-element.30.pack_a), channel_id=1, source_target_pairs={{0,1},{2,3},{4,5},{6,7},{1,0},{3,2},{5,4},{7,6},{8,9},{10,11},{12,... | collective-permute-start | bytes 196616 | tf_op jit(solution)/shard_map/ppermute | solution.py:633
  10.9 3.6 %collective-permute-start.3 = (f32[128,128]{1,0:T(8,128)S(1)}, f32[128,128]{1,0:T(8,128)S(1)}, u32[]{:S(2)}, u32[]{:S(2)}) collective-permute-start(f32[128,128]{1,0:T(8,128)S(1)} %get-tuple-element.31.pack_b), channel_id=1, source_target_pairs={{1,2},{3,4},{5,6},{2,1},{4,3},{6,5},{9,10},{11,12},{13,14},{10,9},... | collective-permute-start | bytes 196616 | tf_op jit(solution)/shard_map/ppermute | solution.py:633
  21.2 28.0 %collective-permute-start.4 = (f32[128,128]{1,0:T(8,128)S(1)}, f32[128,128]{1,0:T(8,128)S(1)}, u32[]{:S(2)}, u32[]{:S(2)}) collective-permute-start(f32[128,128]{1,0:T(8,128)S(1)} %get-tuple-element.44), channel_id=1, source_target_pairs={{0,1},{1,2},{2,3},{3,4},{4,5},{5,6},{6,7},{8,9},{9,10},{10,11},{11... | collective-permute-start | bytes 196616 | tf_op jit(solution)/shard_map/ppermute | solution.py:638
  77.3 16.3 %collective-permute-start.5 = (f32[512,128]{1,0:T(8,128)S(1)}, f32[512,128]{1,0:T(8,128)S(1)}, u32[]{:S(2)}, u32[]{:S(2)}) collective-permute-start(f32[512,128]{1,0:T(8,128)S(1)} %get-tuple-element.49), channel_id=1, source_target_pairs={{0,8},{16,24},{32,40},{48,56},{64,72},{80,88},{96,104},{112,120},{... | collective-permute-start | bytes 786440 | tf_op jit(solution)/shard_map/ppermute | solution.py:633
  77.8 15.9 %collective-permute-start.6 = (f32[512,128]{1,0:T(8,128)S(1)}, f32[512,128]{1,0:T(8,128)S(1)}, u32[]{:S(2)}, u32[]{:S(2)}) collective-permute-start(f32[512,128]{1,0:T(8,128)S(1)} %get-tuple-element.50), channel_id=1, source_target_pairs={{8,16},{24,32},{40,48},{56,64},{72,80},{88,96},{104,112},{16,8},{3... | collective-permute-start | bytes 786440 | tf_op jit(solution)/shard_map/ppermute | solution.py:633

commit v3 on v2

--- a/solution.py
+++ b/solution.py
@@ -48,6 +48,10 @@
 def lane_table(table, n):
     row = jnp.concatenate([table[n : n + 1, :], jnp.zeros((1, 112), F32)], axis=1)
     return jnp.broadcast_to(row, (8, 128))
+
+
+def here():
+    return lax.axis_index("narrow"), lax.axis_size("narrow"), lax.axis_index("wide")
 
 
 def spread(tile, lane):
@@ -70,8 +74,9 @@
 
 
 def faces_kernel(
-    place, sat_in, press_in, rock_in, sat, press, kinds, face_a, face_b, pack_a, pack_b, rock, sem
+    sat_in, press_in, rock_in, sat, press, kinds, face_a, face_b, pack_a, pack_b, rock, sem
 ):
+    place = here()
     lane = lane_iota()
     depth, rows_all, _ = sat.shape
     groups = 8
@@ -135,9 +140,10 @@
 
 
 def lookup_kernel(
-    bricks, place, table, kinds, sat, pack_a, pack_b, columns, rates, residual,
+    bricks, table, kinds, sat, pack_a, pack_b, columns, rates, residual,
     perm, wgain, ogain, frac, own_a, own_b, source, rest,
 ):
+    place = here()
     depth, rows_all, cols = sat.shape
     tables = [lane_table(table, n) for n in range(3)]
     entries = [jnp.broadcast_to(table[2:3, m : m + 1], (8, 128)) for m in range(16)]
@@ -201,9 +207,10 @@
 
 
 def flow_kernel(
-    place, table, press, perm, frac, face_a, face_b, own_a, own_b, got_a, got_b,
+    table, press, perm, frac, face_a, face_b, own_a, own_b, got_a, got_b,
     source, rest, net, ahead, message, qp, wp, rq, rw,
 ):
+    place = here()
     lane = lane_iota()
     sub = sub_iota()
     depth, rows_all, _ = perm.shape
@@ -299,9 +306,10 @@
 
 
 def update_kernel(
-    place, gathered, table, sat, net, source, perm, wgain, ogain, got_a, got_b, beside,
+    gathered, table, sat, net, source, perm, wgain, ogain, got_a, got_b, beside,
     new, chunks, cell_sum, row_sum, col_sum,
 ):
+    place = here()
     lane = lane_iota()
     depth, rows_all, _ = sat.shape
     tiles = rows_all // 8
@@ -366,8 +374,9 @@
 
 
 def relax_kernel(
-    depth, place, got, residual, new, values, row_a, row_b, message, new_out, fd, fr, fc, gain, base, sem
+    depth, got, residual, new, values, row_a, row_b, message, new_out, fd, fr, fc, gain, base, sem
 ):
+    place = here()
     leave = pltpu.make_async_copy(new, new_out, sem.at[0])
     leave.start()
     lane = lane_iota()
@@ -489,7 +498,8 @@
     leave.wait()
 
 
-def coarse_kernel(count, place, news, gathered, out):
+def coarse_kernel(count, news, gathered, out):
+    place = here()
     lane = lane_iota()
     sub = sub_iota()
     inside = lane < count
@@ -571,7 +581,8 @@
     out[...] = lane_pick(mine, place[2])
 
 
-def final_kernel(depth, place, got, values, row_a, row_b, news, coarse, result, packs, out, sem):
+def final_kernel(depth, got, values, row_a, row_b, news, coarse, result, packs, out, sem):
+    place = here()
     lane = lane_iota()
     sub = sub_iota()
     layers = out.shape[0] // 8
@@ -644,20 +655,15 @@
     wide, narrow = lax.axis_size("wide"), lax.axis_size("narrow")
     block = (depth, rows_all, cols)
     plane = (rows_all, cols)
-    place = jnp.stack(
-        [lax.axis_index("narrow"), jnp.int32(narrow), lax.axis_index("wide")]
-    ).astype(jnp.int32)
     vmem = pl.BlockSpec(memory_space=pltpu.VMEM)
-    smem = pl.BlockSpec(memory_space=pltpu.SMEM)
     far = pl.BlockSpec(memory_space=pltpu.HBM)
 
     sat, press, kinds, face_a, face_b, pack_a, pack_b = call(
         faces_kernel,
         [block] * 3 + [(3,) + plane] * 2 + [plane] * 2,
         scratch=[pltpu.VMEM(block, jnp.int32), pltpu.SemaphoreType.DMA((24,))],
-        in_specs=[smem] + [far] * 3,
+        in_specs=[far] * 3,
     )(
-        place,
         *(
             pltpu.with_memory_space_constraint(array, pltpu.HBM)
             for array in (saturation, pressure, rock_class)
@@ -666,9 +672,9 @@
     perm, wgain, ogain, frac, own_a, own_b, source, rest = call(
         functools.partial(lookup_kernel, narrow),
         [block] * 4 + [(3,) + plane] * 2 + [plane, (8, 128)],
-        in_specs=[smem] + [vmem] * 8,
+        in_specs=[vmem] * 8,
     )(
-        place, rock_table, kinds, sat, pack_a, pack_b,
+        rock_table, kinds, sat, pack_a, pack_b,
         well_columns.reshape(1, -1), well_rates.reshape(1, -1), residual,
     )
     got_face_a = partners(face_a, "wide", 0)
@@ -679,9 +685,9 @@
         flow_kernel,
         [block, plane, (wide * narrow, 128)],
         scratch=[pltpu.VMEM(plane, F32)] * 2 + [pltpu.VMEM((depth, 8, cols), F32)] * 2,
-        in_specs=[smem] + [vmem] * 12,
+        in_specs=[vmem] * 12,
     )(
-        place, rock_table, press, perm, frac, got_face_a, got_face_b, own_a, own_b,
+        rock_table, press, perm, frac, got_face_a, got_face_b, own_a, own_b,
         got_pack_a, got_pack_b, source, rest,
     )
     beside = forward(ahead, "narrow")
@@ -691,9 +697,9 @@
         update_kernel,
         [block, (chunk_rows, 128)],
         scratch=[pltpu.VMEM(plane, F32)] * 3,
-        in_specs=[smem] + [vmem] * 11,
+        in_specs=[vmem] * 11,
     )(
-        place, gathered, rock_table, sat, net, source, perm, wgain, ogain, got_pack_a, got_pack_b,
+        gathered, rock_table, sat, net, source, perm, wgain, ogain, got_pack_a, got_pack_b,
         beside,
     )
     got = lax.all_to_all(chunks, "wide", 0, 0, tiled=True)
@@ -702,15 +708,15 @@
         functools.partial(relax_kernel, depth),
         [(layers * 8 + 64, 128)] + [(2 * layers, 128)] * 2 + [(message_rows, 128), block],
         scratch=[pltpu.VMEM((layers * 8 + 64, 128), F32)] * 5 + [pltpu.SemaphoreType.DMA((1,))],
-        in_specs=[smem] + [vmem] * 3,
+        in_specs=[vmem] * 3,
         out_specs=[vmem] * 4 + [far],
-    )(place, got, residual.reshape(layers * 8, 128), new)
+    )(got, residual.reshape(layers * 8, 128), new)
     got_row_a = partners(row_a, "wide", 0)
     got_row_b = partners(row_b, "wide", 1)
     news = lax.all_to_all(message, "narrow", 0, 0, tiled=True)
     (coarse,) = call(
-        functools.partial(coarse_kernel, wide), [(8, 128)], in_specs=[smem, vmem, vmem]
-    )(place, news, gathered)
+        functools.partial(coarse_kernel, wide), [(8, 128)], in_specs=[vmem, vmem]
+    )(news, gathered)
     (precond,) = call(
         functools.partial(final_kernel, depth),
         [(layers * 8, 128)],
@@ -719,9 +725,9 @@
             pltpu.VMEM((layers * 8, 128), F32),
             pltpu.SemaphoreType.DMA((layers // 64,)),
         ],
-        in_specs=[smem] + [vmem] * 6,
+        in_specs=[vmem] * 6,
         out_specs=[far],
-    )(place, got, values, got_row_a, got_row_b, news, coarse)
+    )(got, values, got_row_a, got_row_b, news, coarse)
     return (sat_new, precond.reshape(layers, brick_rows, cols))
 
 

time: 96.1 us -> 92.7 us (0.965)
  Pallas kernels: 25.1 us -> 21.3 us
    pallas_call x7, Pallas kernels: 25.1 us -> 21.3 us  [run(): pl.pallas_call(kernel, out_shape=[jax.ShapeDtypeStruct(shape, F32) for sh...]
  transfers between devices with their start and end apart: 7 -> 7, of which waited for: 0 -> 1; matrix products, arithmetic and copies ran while one was open for 0% -> 0% of each run, Pallas kernels for 5% -> 4%
where the time goes in v3:
time: 92.7 us; the launch traced here: 92.5 us
  blocking collectives  55.1 us (59%)
  Pallas kernels  21.3 us (23%)
  starting transfers between devices  15 us (16%)
    all_to_all x1, blocking collectives, shards(): gathered = lax.all_to_all(message, ('wide', 'narrow'), 0, 0, tiled=True)  23.1 us
    pallas_call x7, Pallas kernels, run(): pl.pallas_call(kernel, out_shape=[jax.ShapeDtypeStruct(shape, F32) for sh...  21.3 us
    all_to_all x1, blocking collectives, shards(): got = lax.all_to_all(chunks, 'wide', 0, 0, tiled=True)  20.1 us
    all_to_all x1, blocking collectives, shards(): news = lax.all_to_all(message, 'narrow', 0, 0, tiled=True)  11.9 us
    ppermute x6, starting transfers between devices, partners(): return lax.ppermute(array, axis, pairs + [(j, i) for i, j in pairs])  9.77 us
    ppermute x1, starting transfers between devices, forward(): return lax.ppermute(array, axis, [(i, i + 1) for i in range(count - 1)])  5.23 us
  transfers between devices with their start and end apart: 7, of which 1 were waited for; matrix products, arithmetic and copies ran while one was open for 0% of the time, Pallas kernels for 4%

profile of v3, /device:TPU:1, one launch (start us, length us, event | category | flops | bytes accessed | tf_op | source)
XLA Modules:
  0.0 92.5 jit_solution(14706122455531057777)
XLA Ops:
  0.7 3.3 %shard_map.86 = (f32[16,128,128]{2,1,0:T(8,128)S(1)}, f32[16,128,128]{2,1,0:T(8,128)S(1)}, f32[16,128,128]{2,1,0:T(8,128)S(1)}, f32[3,128,128]{2,1,0:T(8,128)S(1...) custom-call(f32[16,128,128]{2,1,0:T(8,128)} %sat_in.1, f32[16,128,128]{2,1,0:T(8,128)} %press_in.1, ...), custom_call_target="tpu_custom_call" | custom-call | tf_op jit(solution)/shard_map/pallas_call | solution.py:63
  3.9 1.5 %collective-permute-start = (f32[3,128,128]{2,1,0:T(8,128)S(1)}, f32[3,128,128]{2,1,0:T(8,128)S(1)}, u32[]{:S(2)}, u32[]{:S(2)}) collective-permute-start(f32[3,128,128]{2,1,0:T(8,128)S(1)} %get-tuple-element.34), channel_id=1, source_target_pairs={{0,8},{16,24},{32,40},{48,56},{64,72},{80,88},{96,104},{112,120},{... | collective-permute-start | bytes 589832 | tf_op jit(solution)/shard_map/ppermute | solution.py:644
  5.4 3.6 %collective-permute-start.1 = (f32[3,128,128]{2,1,0:T(8,128)S(1)}, f32[3,128,128]{2,1,0:T(8,128)S(1)}, u32[]{:S(2)}, u32[]{:S(2)}) collective-permute-start(f32[3,128,128]{2,1,0:T(8,128)S(1)} %get-tuple-element.35), channel_id=1, source_target_pairs={{8,16},{24,32},{40,48},{56,64},{72,80},{88,96},{104,112},{16,8},{3... | collective-permute-start | bytes 589832 | tf_op jit(solution)/shard_map/ppermute | solution.py:644
  9.0 1.4 %collective-permute-start.2 = (f32[128,128]{1,0:T(8,128)S(1)}, f32[128,128]{1,0:T(8,128)S(1)}, u32[]{:S(2)}, u32[]{:S(2)}) collective-permute-start(f32[128,128]{1,0:T(8,128)S(1)} %get-tuple-element.30.pack_a), channel_id=1, source_target_pairs={{0,1},{2,3},{4,5},{6,7},{1,0},{3,2},{5,4},{7,6},{8,9},{10,11},{12,... | collective-permute-start | bytes 196616 | tf_op jit(solution)/shard_map/ppermute | solution.py:644
  10.3 0.7 collective-permute-start.3
  11.0 2.4 %shard_map.87 = (f32[16,128,128]{2,1,0:T(8,128)S(1)}, f32[16,128,128]{2,1,0:T(8,128)S(1)}, f32[16,128,128]{2,1,0:T(8,128)S(1)}, f32[16,128,128]{2,1,0:T(8,128)S(...) custom-call(f32[3,16]{1,0:T(4,128)S(1)} %copy-done.1, ...), custom_call_target="tpu_custom_call" | custom-call | tf_op jit(solution)/shard_map/pallas_call | solution.py:63
  13.4 0.0 collective-permute-done.2.got_a
  13.4 0.0 collective-permute-done.3.got_b
  13.4 0.0 collective-permute-done.face_a
  13.4 0.2 collective-permute-done.1.face_b
  13.7 6.2 %shard_map.88 = (f32[16,128,128]{2,1,0:T(8,128)S(1)}, f32[128,128]{1,0:T(8,128)S(1)}, f32[128,128]{1,0:T(8,128)S(1)}) custom-call(f32[3,16]{1,0:T(4,128)S(1)} %copy-done.1, f32[16,128,128]{2,1,0:T(8,128)S(1)} %get-tuple-element.27.press, f32[16,128,128]{2,1,0:T(8,128)S(1)} %get-tuple-element.32.perm, f32[16,128,128]{2,1,0:T(8,128)S(1)} %get-tuple-element.33.frac, ...), custom_call_target="tpu_custom_call" | custom-call | tf_op jit(solution)/shard_map/pallas_call | solution.py:63
  19.8 5.2 %collective-permute-start.4 = (f32[128,128]{1,0:T(8,128)S(1)}, f32[128,128]{1,0:T(8,128)S(1)}, u32[]{:S(2)}, u32[]{:S(2)}) collective-permute-start(f32[128,128]{1,0:T(8,128)S(1)} %get-tuple-element.44), channel_id=1, source_target_pairs={{0,1},{1,2},{2,3},{3,4},{4,5},{5,6},{6,7},{8,9},{9,10},{10,11},{11... | collective-permute-start | bytes 196616 | tf_op jit(solution)/shard_map/ppermute | solution.py:649
  25.1 23.1 %all_to_all.33 = f32[128,1,128]{2,1,0:T(1,128)S(1)} all-to-all(f32[128,1,128]{2,1,0:T(1,128)S(1)} %bitcast.21), channel_id=1, replica_groups=mesh['wide'=16,'narrow'=8] {'wide','narrow'}, dimensions={0} | all-to-all | bytes 131072 | tf_op jit(solution)/shard_map/all_to_all | solution.py:694
  48.2 0.0 collective-permute-done.4.beside
  48.2 1.0 %shard_map.89 = (f32[16,128,128]{2,1,0:T(8,128)S(1)}, f32[2176,128]{1,0:T(8,128)S(1)}) custom-call(f32[128,128]{1,0:T(8,128)S(1)} %bitcast.18, f32[3,16]{1,0:T(4,128)S(1)} %copy-done.1, f32[16,128,128]{2,1,0:T(8,128)S(1)} %get-tuple-element.29.sat, f32[16,128,128]{2,1,0:T(8,128)S(1)} %get-tuple-element.41.net, f32[128,128]{1,0:T(8,128)S(1)} %get-tuple-element.38.source, ...), custom_call_target="tpu_custom_call" | custom-call | tf_op jit(solution)/shard_map/pallas_call | solution.py:63
  49.2 20.1 %all_to_all.34 = f32[16,136,128]{2,1,0:T(8,128)S(1)} all-to-all(f32[16,136,128]{2,1,0:T(8,128)S(1)} %bitcast.17), channel_id=1, replica_groups=mesh['wide'=16,'narrow'=8] {'wide'}, dimensions={0} | all-to-all | bytes 2228224 | tf_op jit(solution)/shard_map/all_to_all | solution.py:705
  69.4 5.7 %shard_map.90 = (f32[2112,128]{1,0:T(8,128)S(1)}, f32[512,128]{1,0:T(8,128)S(1)}, f32[512,128]{1,0:T(8,128)S(1)}, f32[576,128]{1,0:T(8,128)S(1)}, f32[16,128,128]{2,1,0:T(8,128)}) custom-call(f32[2176,128]{1,0:T(8,128)S(1)} %bitcast.12, f32[2048,128]{1,0:T(8,128)S(1)} %bitcast.14, f32[16,128,128]{2,1,0:T(8,128)S(1)} %get-tuple-element.46.new), custom_call_target="tpu_custom_call" | custom-call | tf_op jit(solution)/shard_map/pallas_call | solution.py:63
  75.1 0.5 collective-permute-start.5
  75.5 2.3 %collective-permute-start.6 = (f32[512,128]{1,0:T(8,128)S(1)}, f32[512,128]{1,0:T(8,128)S(1)}, u32[]{:S(2)}, u32[]{:S(2)}) collective-permute-start(f32[512,128]{1,0:T(8,128)S(1)} %get-tuple-element.50), channel_id=1, source_target_pairs={{8,16},{24,32},{40,48},{56,64},{72,80},{88,96},{104,112},{16,8},{3... | collective-permute-start | bytes 786440 | tf_op jit(solution)/shard_map/ppermute | solution.py:644
  77.8 11.9 %all_to_all.35 = f32[8,72,128]{2,1,0:T(8,128)S(1)} all-to-all(f32[8,72,128]{2,1,0:T(8,128)S(1)} %bitcast.20), channel_id=1, replica_groups=mesh['wide'=16,'narrow'=8] {'narrow'}, dimensions={0} | all-to-all | bytes 589824 | tf_op jit(solution)/shard_map/all_to_all | solution.py:716
  89.7 1.2 %shard_map.91.coarse = f32[8,128]{1,0:T(8,128)S(1)} custom-call(f32[576,128]{1,0:T(8,128)S(1)} %bitcast.15, f32[128,128]{1,0:T(8,128)S(1)} %bitcast.19), custom_call_target="tpu_custom_call" | custom-call | tf_op jit(solution)/shard_map/pallas_call | solution.py:63
  90.9 0.0 collective-permute-done.5.row_a
  90.9 0.0 collective-permute-done.6.row_b
  90.9 1.6 %shard_map.92 = f32[2048,128]{1,0:T(8,128)} custom-call(f32[2176,128]{1,0:T(8,128)S(1)} %bitcast.13, f32[2112,128]{1,0:T(8,128)S(1)} %get-tuple-element.48.values, f32[512,128]{1,0:T(8,128)S(1)} %collective-permute-done.5.row_a, f32[512,128]{1,0:T(8,128)S(1)} %collective-permute-done.6.row_b, f32[576,128]{1,0:T(8,128)S(1)} %bitcast.16, ...), custom_call_target="tpu_custom_call" | custom-call | tf_op jit(solution)/shard_map/pallas_call | solution.py:63
  (8 shorter events, 0.0 us)
Async XLA Ops:
  0.6 10.4 %copy-start.1 = (f32[3,16]{1,0:T(4,128)S(1)}, f32[3,16]{1,0:T(4,128)}, u32[]{:S(2)}) copy-start(f32[3,16]{1,0:T(4,128)} %table.5) | copy-start | bytes 580
  0.6 10.4 %copy-start = (f32[256,8,128]{2,1,0:T(8,128)S(1)}, f32[256,8,128]{2,1,0:T(8,128)}, u32[]{:S(2)}) copy-start(f32[256,8,128]{2,1,0:T(8,128)} %residual.1) | copy-start | bytes 3145732
  0.7 10.4 %copy-start.3 = (f32[64]{0:T(128)S(1)}, f32[64]{0:T(128)}, u32[]{:S(2)}) copy-start(f32[64]{0:T(128)} %param.12) | copy-start | bytes 772
  0.7 10.4 %copy-start.2 = (s32[64]{0:T(128)S(1)}, s32[64]{0:T(128)}, u32[]{:S(2)}) copy-start(s32[64]{0:T(128)} %param.11) | copy-start | bytes 772
  3.9 9.5 %collective-permute-start = (f32[3,128,128]{2,1,0:T(8,128)S(1)}, f32[3,128,128]{2,1,0:T(8,128)S(1)}, u32[]{:S(2)}, u32[]{:S(2)}) collective-permute-start(f32[3,128,128]{2,1,0:T(8,128)S(1)} %get-tuple-element.34), channel_id=1, source_target_pairs={{0,8},{16,24},{32,40},{48,56},{64,72},{80,88},{96,104},{112,120},{... | collective-permute-start | bytes 589832 | tf_op jit(solution)/shard_map/ppermute | solution.py:644
  5.4 8.3 %collective-permute-start.1 = (f32[3,128,128]{2,1,0:T(8,128)S(1)}, f32[3,128,128]{2,1,0:T(8,128)S(1)}, u32[]{:S(2)}, u32[]{:S(2)}) collective-permute-start(f32[3,128,128]{2,1,0:T(8,128)S(1)} %get-tuple-element.35), channel_id=1, source_target_pairs={{8,16},{24,32},{40,48},{56,64},{72,80},{88,96},{104,112},{16,8},{3... | collective-permute-start | bytes 589832 | tf_op jit(solution)/shard_map/ppermute | solution.py:644
  9.0 4.4 %collective-permute-start.2 = (f32[128,128]{1,0:T(8,128)S(1)}, f32[128,128]{1,0:T(8,128)S(1)}, u32[]{:S(2)}, u32[]{:S(2)}) collective-permute-start(f32[128,128]{1,0:T(8,128)S(1)} %get-tuple-element.30.pack_a), channel_id=1, source_target_pairs={{0,1},{2,3},{4,5},{6,7},{1,0},{3,2},{5,4},{7,6},{8,9},{10,11},{12,... | collective-permute-start | bytes 196616 | tf_op jit(solution)/shard_map/ppermute | solution.py:644
  10.3 3.1 %collective-permute-start.3 = (f32[128,128]{1,0:T(8,128)S(1)}, f32[128,128]{1,0:T(8,128)S(1)}, u32[]{:S(2)}, u32[]{:S(2)}) collective-permute-start(f32[128,128]{1,0:T(8,128)S(1)} %get-tuple-element.31.pack_b), channel_id=1, source_target_pairs={{1,2},{3,4},{5,6},{2,1},{4,3},{6,5},{9,10},{11,12},{13,14},{10,9},... | collective-permute-start | bytes 196616 | tf_op jit(solution)/shard_map/ppermute | solution.py:644
  19.8 28.4 %collective-permute-start.4 = (f32[128,128]{1,0:T(8,128)S(1)}, f32[128,128]{1,0:T(8,128)S(1)}, u32[]{:S(2)}, u32[]{:S(2)}) collective-permute-start(f32[128,128]{1,0:T(8,128)S(1)} %get-tuple-element.44), channel_id=1, source_target_pairs={{0,1},{1,2},{2,3},{3,4},{4,5},{5,6},{6,7},{8,9},{9,10},{10,11},{11... | collective-permute-start | bytes 196616 | tf_op jit(solution)/shard_map/ppermute | solution.py:649
  75.1 15.8 %collective-permute-start.5 = (f32[512,128]{1,0:T(8,128)S(1)}, f32[512,128]{1,0:T(8,128)S(1)}, u32[]{:S(2)}, u32[]{:S(2)}) collective-permute-start(f32[512,128]{1,0:T(8,128)S(1)} %get-tuple-element.49), channel_id=1, source_target_pairs={{0,8},{16,24},{32,40},{48,56},{64,72},{80,88},{96,104},{112,120},{... | collective-permute-start | bytes 786440 | tf_op jit(solution)/shard_map/ppermute | solution.py:644
  75.5 15.3 %collective-permute-start.6 = (f32[512,128]{1,0:T(8,128)S(1)}, f32[512,128]{1,0:T(8,128)S(1)}, u32[]{:S(2)}, u32[]{:S(2)}) collective-permute-start(f32[512,128]{1,0:T(8,128)S(1)} %get-tuple-element.50), channel_id=1, source_target_pairs={{8,16},{24,32},{40,48},{56,64},{72,80},{88,96},{104,112},{16,8},{3... | collective-permute-start | bytes 786440 | tf_op jit(solution)/shard_map/ppermute | solution.py:644
